TPU v7x, 32 devices: a whole 2x2x4 slice. The times are simulated.
32 devices in a mesh: tok: 16 (over z, y, x), mdl: 2 (over core).
Axes of the slice: x: 2, y: 2, z: 4, core: 2. Of those that a mesh axis runs over, the one named last changes fastest.
Arguments:
- tokens: bfloat16 [64, 64, 768], P('tok'), may hold values from -6 to 6
- cotangent: bfloat16 [64, 64, 768], P('tok'), may hold values from -6 to 6
- norm_gain: float32 [768], replicated, may hold values from 0.5 to 1.5
- w_qkv: bfloat16 [768, 1536], P(None, 'mdl'), may hold values from -0.21875 to 0.21875
- w_out: bfloat16 [512, 768], P('mdl'), may hold values from -0.25 to 0.25
- w_up: bfloat16 [768, 3072], P(None, 'mdl'), may hold values from -0.21875 to 0.21875
- w_down: bfloat16 [3072, 768], P('mdl'), may hold values from -0.109375 to 0.109375
- w_disp: bfloat16 [768, 192], replicated, may hold values from -0.21875 to 0.21875
- rel_bias: float32 [8, 64, 448], P('mdl'), may hold values from -4 to 304
- face_source: int32 [64, 6], P('tok'), may hold values from 0 to 15, all different within a row; in each aligned block of 4 rows (0 to 3, 4 to 7, ...) at most 2 rows name the same one
- face_live: int32 [64, 6], P('tok'), may hold values 0 or 1
- send_bricks: int32 [16, 16, 2], P('tok'), may hold values from 0 to 3
Outputs:
- folding: float32 [64, 64], P('tok')
- grad_tokens: bfloat16 [64, 64, 768], P('tok')
- grad_wqkv: float32 [768, 1536], P('tok', 'mdl')
Inputs may be any that keep to these rules, and one draw needn't show every extreme that they name: `face_source`: entry [b, j] names the device whose message carries the j-th face neighbour of brick b; the entries of a row differ; among the rows of one device no device is named more than 2 times, and that count is reached in every draw.
All inputs are finite; a program needn't handle non-finite values. No bound on the sum of `face_live` on one device may be relied on, other than what follows from the above.
Results may differ from a plain program's by a relative error of at most 0.015.
Values may be sent and summed in bfloat16 or wider, within the bound.
A program may use at most 64 MiB of HBM per device.

v0:
```python
import math

import jax
import jax.numpy as jnp
from jax import lax
from jax.sharding import PartitionSpec as P

fold_weight = 8.0
norm_eps = 1e-05


def fold_of(displace):
    grid_field = displace.reshape(displace.shape[0], 3, 4, 4, 4)
    corner = grid_field[:, :, :3, :3, :3]
    slope_x = grid_field[:, :, :3, :3, 1:] - corner
    slope_y = grid_field[:, :, :3, 1:, :3] - corner
    slope_z = grid_field[:, :, 1:, :3, :3] - corner
    slopes = (slope_x, slope_y, slope_z)
    jacobian = [
        [slopes[across][:, target] + (1.0 if target == across else 0.0) for across in range(3)]
        for target in range(3)
    ]
    determinant = (
        jacobian[0][0] * (jacobian[1][1] * jacobian[2][2] - jacobian[1][2] * jacobian[2][1])
        - jacobian[0][1] * (jacobian[1][0] * jacobian[2][2] - jacobian[1][2] * jacobian[2][0])
        + jacobian[0][2] * (jacobian[1][0] * jacobian[2][1] - jacobian[1][1] * jacobian[2][0])
    )
    return jnp.mean(jax.nn.softplus(-determinant), axis=(1, 2, 3))


def gelu_tanh(value):
    return jax.nn.gelu(value, approximate=True)


def body(
    tokens,
    cotangent,
    norm_gain,
    w_qkv,
    w_out,
    w_up,
    w_down,
    w_disp,
    rel_bias,
    face_source,
    face_live,
    send_bricks,
):
    own_bricks, per_brick, model_width = tokens.shape
    row_count = own_bricks * per_brick
    head_count = rel_bias.shape[0]
    head_size = w_out.shape[0] // head_count
    face_count = face_source.shape[1]
    window_count = face_count + 1
    device_count = lax.axis_size("tok")
    slot_count = send_bricks.shape[2]
    slot_total = device_count * slot_count
    pair_width = head_count * 2 * head_size
    score_scale = 1.0 / math.sqrt(head_size)
    inputs = tokens.astype(jnp.float32)
    inverse = lax.rsqrt(jnp.mean(inputs * inputs, axis=-1, keepdims=True) + norm_eps)
    normed = inputs * inverse
    hidden = (normed * norm_gain).astype(jnp.bfloat16).reshape(row_count, model_width)
    packed = jnp.dot(hidden, w_qkv, preferred_element_type=jnp.float32).astype(jnp.bfloat16)
    packed = packed.reshape(own_bricks, per_brick, head_count, 3, head_size)
    queries = packed[:, :, :, 0]
    own_pairs = packed[:, :, :, 1:]
    keyval = own_pairs.reshape(own_bricks, per_brick, pair_width)
    outgoing = keyval[send_bricks[0]]
    sources = face_source.reshape(-1)
    matches = (sources[:, None] == jnp.arange(device_count, dtype=jnp.int32)[None, :]).astype(
        jnp.int32
    )
    earlier = jnp.cumsum(matches, axis=0) - matches
    slot_index = jnp.sum(earlier * matches, axis=1)
    arrival = sources * slot_count + slot_index
    visible = jnp.concatenate([jnp.ones((own_bricks, 1), jnp.int32), face_live], axis=1) > 0
    visible = jnp.repeat(visible, per_brick, axis=1)
    incoming = lax.all_to_all(outgoing, "tok", split_axis=0, concat_axis=0, tiled=True)
    remote = incoming.reshape(slot_total, per_brick, pair_width)[arrival]
    remote = remote.reshape(own_bricks, face_count * per_brick, head_count, 2, head_size)
    windows = jnp.concatenate([own_pairs, remote], axis=1)
    key_rows = windows[:, :, :, 0]
    value_rows = windows[:, :, :, 1]
    raw_scores = jnp.einsum(
        "bqhd,bkhd->bhqk", queries, key_rows, preferred_element_type=jnp.float32
    )
    scores = raw_scores * score_scale + rel_bias[None]
    scores = jnp.where(visible[:, None, None, :], scores, -1000000000.0)
    row_max = jnp.max(scores, axis=-1, keepdims=True)
    exponent = jnp.exp(scores - row_max)
    probability = exponent / jnp.sum(exponent, axis=-1, keepdims=True)
    weights = probability.astype(jnp.bfloat16)
    attended = jnp.einsum(
        "bhqk,bkhd->bqhd", weights, value_rows, preferred_element_type=jnp.float32
    ).astype(jnp.bfloat16)
    attended = attended.reshape(row_count, head_count * head_size)
    up_pre = jnp.dot(hidden, w_up, preferred_element_type=jnp.float32)
    activ = gelu_tanh(up_pre).astype(jnp.bfloat16)
    partial_out = jnp.dot(attended, w_out, preferred_element_type=jnp.float32) + jnp.dot(
        activ, w_down, preferred_element_type=jnp.float32
    )
    flat_inputs = inputs.reshape(row_count, model_width)
    total_out = lax.psum(partial_out, "mdl")
    layer_out = (flat_inputs + total_out).astype(jnp.bfloat16)
    displace = jnp.dot(layer_out, w_disp, preferred_element_type=jnp.float32)
    folding, fold_back = jax.vjp(fold_of, displace)
    grad_disp = fold_back(jnp.full_like(folding, fold_weight))[0].astype(jnp.bfloat16)
    grad_out = (
        cotangent.reshape(row_count, model_width).astype(jnp.float32)
        + jnp.dot(grad_disp, w_disp.T, preferred_element_type=jnp.float32)
    ).astype(jnp.bfloat16)
    grad_act = jnp.dot(grad_out, w_down.T, preferred_element_type=jnp.float32)
    _, gelu_back = jax.vjp(gelu_tanh, up_pre)
    grad_pre = gelu_back(grad_act)[0].astype(jnp.bfloat16)
    grad_mixed = jnp.dot(grad_out, w_out.T, preferred_element_type=jnp.float32).astype(jnp.bfloat16)
    grad_mixed = grad_mixed.reshape(own_bricks, per_brick, head_count, head_size)
    grad_probs = jnp.einsum(
        "bqhd,bkhd->bhqk", grad_mixed, value_rows, preferred_element_type=jnp.float32
    )
    grad_scores = probability * (
        grad_probs - jnp.sum(probability * grad_probs, axis=-1, keepdims=True)
    )
    grad_low = grad_scores.astype(jnp.bfloat16)
    grad_query = (
        jnp.einsum("bhqk,bkhd->bqhd", grad_low, key_rows, preferred_element_type=jnp.float32)
        * score_scale
    )
    selector = (
        send_bricks[0].reshape(-1)[None, :] == jnp.arange(own_bricks, dtype=jnp.int32)[:, None]
    ).astype(jnp.float32)
    grad_key = (
        jnp.einsum("bhqk,bqhd->bkhd", grad_low, queries, preferred_element_type=jnp.float32)
        * score_scale
    )
    grad_value = jnp.einsum(
        "bhqk,bqhd->bkhd", weights, grad_mixed, preferred_element_type=jnp.float32
    )
    grad_window = jnp.stack([grad_key, grad_value], axis=3).reshape(
        own_bricks, window_count, per_brick, pair_width
    )
    grad_own = grad_window[:, 0]
    grad_far = grad_window[:, 1:].reshape(own_bricks * face_count, per_brick, pair_width)
    returning = (
        jnp.zeros((slot_total, per_brick, pair_width), jnp.float32).at[arrival].add(grad_far)
    )
    returning = returning.reshape(device_count, slot_count, per_brick, pair_width)
    returned = lax.all_to_all(
        returning.astype(jnp.bfloat16), "tok", split_axis=0, concat_axis=0, tiled=True
    ).astype(returning.dtype)
    returned_rows = returned.reshape(slot_total, per_brick * pair_width)
    grad_sent = jnp.dot(
        selector, returned_rows, precision=lax.Precision.HIGHEST, preferred_element_type=jnp.float32
    )
    grad_keyval = grad_own + grad_sent.reshape(own_bricks, per_brick, pair_width)
    grad_keyval = grad_keyval.reshape(own_bricks, per_brick, head_count, 2, head_size)
    grad_packed = jnp.concatenate([grad_query[:, :, :, None], grad_keyval], axis=3).astype(
        jnp.bfloat16
    )
    grad_packed = grad_packed.reshape(row_count, head_count * 3 * head_size)
    grad_part = jnp.dot(grad_packed, w_qkv.T, preferred_element_type=jnp.float32) + jnp.dot(
        grad_pre, w_up.T, preferred_element_type=jnp.float32
    )
    grad_hidden = lax.psum(grad_part.astype(jnp.bfloat16), "mdl").astype(jnp.float32)
    grad_normed = grad_hidden.reshape(own_bricks, per_brick, model_width) * norm_gain
    grad_inputs = grad_out.reshape(own_bricks, per_brick, model_width).astype(
        jnp.float32
    ) + inverse * (grad_normed - normed * jnp.mean(grad_normed * normed, axis=-1, keepdims=True))
    grad_weight = lax.psum_scatter(
        jnp.dot(hidden.T, grad_packed, preferred_element_type=jnp.float32),
        "tok",
        scatter_dimension=0,
        tiled=True,
    )
    return (folding.reshape(own_bricks, per_brick), grad_inputs.astype(jnp.bfloat16), grad_weight)


def solution(mesh):
    return jax.shard_map(
        body,
        mesh=mesh,
        in_specs=(
            P("tok", None, None),
            P("tok", None, None),
            P(),
            P(None, "mdl"),
            P("mdl", None),
            P(None, "mdl"),
            P("mdl", None),
            P(),
            P("mdl", None, None),
            P("tok", None),
            P("tok", None),
            P("tok", None, None),
        ),
        out_specs=(P("tok", None), P("tok", None, None), P("tok", "mdl")),
        check_vma=False,
    )
```

profile of v0, /device:TPU:0, one launch (start us, length us, event | category | flops | bytes accessed | tf_op | source)
XLA Modules:
  0.0 420.4 jit_solution(1245665591545457448)
XLA Ops:
  10.5 2.6 convolution_convert_fusion
  19.1 8.5 %all-to-all-start = ((bf16[16,2,64,512]{3,2,1,0:T(8,128)(2,1)}), bf16[16,2,64,512]{3,2,1,0:T(8,128)(2,1)}, u32[]{:S(2)}, u32[]{:S(2)}) async-start(bf16[16,2,64,512]{3,2,1,0:T(8,128)(2,1)} %bitcast.142), calls=%async_computation | async-start | bytes 4194304 | tf_op jit(solution)/shard_map/all_to_all | solution.py:79
  31.6 39.2 %all-to-all-done = bf16[16,2,64,512]{3,2,1,0:T(8,128)(2,1)} async-done(((bf16[16,2,64,512]{3,2,1,0:T(8,128)(2,1)}), bf16[16,2,64,512]{3,2,1,0:T(8,128)(2,1)}, u32[]{:S(2)}, u32[]{:S(2)}) %all-to-all-start) | async-done | bytes 2097184 | tf_op jit(solution)/shard_map/all_to_all | solution.py:79
  70.7 3.4 gather_fusion.1
  74.2 7.0 %reshape.218 = bf16[4,384,4,2,64]{4,3,2,1,0:T(2,128)(2,1)} reshape(bf16[24,64,512]{2,1,0:T(8,128)(2,1)} %gather_fusion.1) | data formatting | bytes 3145728 | tf_op jit(solution)/shard_map/reshape | solution.py:81
  81.2 8.5 %copy.44 = bf16[4,384,4,2,64]{1,4,2,0,3:T(8,128)(2,1)} copy(bf16[4,384,4,2,64]{4,3,2,1,0:T(2,128)(2,1)} %reshape.218) | data formatting | bytes 3145728 | tf_op jit(solution)/shard_map/reshape | solution.py:81
  89.7 3.6 fusion.92
  93.2 3.2 fusion.18
  99.6 4.1 convolution_add_fusion.2
  103.8 23.7 %all-reduce.17.cloned.1.call-done = f32[256,768]{1,0:T(8,128)} async-done(((f32[256,768]{1,0:T(8,128)}), f32[256,768]{1,0:T(8,128)}) %all-reduce.17.cloned.1.call-update) | async-done | bytes 786448 | tf_op jit(solution)/shard_map/psum | solution.py:104
  144.6 2.7 pad_maximum_fusion
  147.2 11.9 %copy.50 = f32[4,448,4,2,64]{4,3,2,1,0:T(2,128)} copy(f32[4,448,4,2,64]{1,4,2,0,3:T(8,128)} %pad_maximum_fusion) | data formatting | bytes 7340032 | tf_op jit(solution)/shard_map/stack | solution.py:139
  159.1 9.5 %reshape.181 = f32[4,7,64,512]{3,2,1,0:T(8,128)} reshape(f32[4,448,4,2,64]{4,3,2,1,0:T(2,128)} %copy.50) | data formatting | bytes 7340032 | tf_op jit(solution)/shard_map/reshape | solution.py:139
  168.6 4.0 slice.98
  175.1 9.6 %scatter_fusion = f32[32,64,512]{2,1,0:T(8,128)} fusion(f32[32,64,512]{2,1,0:T(8,128)} %broadcast_in_dim.28, s32[24]{0:T(128)S(1)} %fusion.67, f32[24,64,512]{2,1,0:T(8,128)} %bitcast.140), kind=kCustom, calls=%fused_computation.2 | custom fusion | flops 786432 | bytes 9437280 | tf_op jit(solution)/shard_map/scatter-add | solution.py:145
  184.8 3.8 convert_element_type.104
  188.6 7.1 %all-to-all-start.1 = ((bf16[16,2,64,512]{3,2,1,0:T(8,128)(2,1)}), bf16[16,2,64,512]{3,2,1,0:T(8,128)(2,1)}, u32[]{:S(2)}, u32[]{:S(2)}) async-start(bf16[16,2,64,512]{3,2,1,0:T(8,128)(2,1)} %bitcast.141), calls=%async_computation.1 | async-start | bytes 4194304 | tf_op jit(solution)/shard_map/all_to_all | solution.py:148
  198.2 40.7 %all-to-all-done.1 = bf16[16,2,64,512]{3,2,1,0:T(8,128)(2,1)} async-done(((bf16[16,2,64,512]{3,2,1,0:T(8,128)(2,1)}), bf16[16,2,64,512]{3,2,1,0:T(8,128)(2,1)}, u32[]{:S(2)}, u32[]{:S(2)}) %all-to-all-start.1) | async-done | bytes 2097184 | tf_op jit(solution)/shard_map/all_to_all | solution.py:148
  239.0 3.8 fusion.14
  248.2 2.7 fusion.102
  250.9 5.2 %fusion.13 = bf16[256,768]{1,0:T(8,128)(2,1)} fusion(f32[256,768]{1,0:T(8,128)} %fusion.102, bf16[768,1536]{1,0:T(8,128)(2,1)S(1)} %copy-done, f32[256,1536]{1,0:T(8,128)} %fusion.100, bf16[256,768]{1,0:T(8,128)(2,1)} %copy-done.7, bf16[1536,768]{1,0:T(8,128)(2,1)} %param.18), kind=kOutput, calls=%fused_computation.32 | convolution fusion | flops 1216217088 | bytes 7864320 | tf_op jit(solution)/shard_map/dot_general | solution.py:161
  256.2 2.9 fusion.103
  259.9 19.6 %all-reduce.19.cloned.1.call-done = bf16[4,64,768]{2,1,0:T(8,128)(2,1)} async-done(((bf16[4,64,768]{2,1,0:T(8,128)(2,1)}), bf16[4,64,768]{2,1,0:T(8,128)(2,1)}) %all-reduce.19.cloned.1.call-update) | async-done | bytes 393232 | tf_op jit(solution)/shard_map/psum | solution.py:164
  282.9 131.0 %reduce-scatter.2.cloned.1.call-done = f32[48,768]{1,0:T(8,128)} async-done(((f32[768,768]{1,0:T(8,128)}), f32[48,768]{1,0:T(8,128)}) %reduce-scatter.2.cloned.1.call-update) | async-done | bytes 147472 | tf_op jit(solution)/shard_map/reduce_scatter | solution.py:169
  (113 shorter events, 47.9 us)
Async XLA Ops:
  7.2 22.4 %copy-start = (bf16[768,1536]{1,0:T(8,128)(2,1)S(1)}, bf16[768,1536]{1,0:T(8,128)(2,1)}, u32[]{:S(2)}) copy-start(bf16[768,1536]{1,0:T(8,128)(2,1)} %param.17) | copy-start | bytes 7077892
  10.5 19.0 %copy-start.3 = (bf16[4,64,768]{2,1,0:T(8,128)(2,1)}, bf16[4,64,768]{2,1,0:T(8,128)(2,1)S(1)}, u32[]{:S(2)}) copy-start(bf16[4,64,768]{2,1,0:T(8,128)(2,1)S(1)} %multiply_convert_fusion.3) | copy-start | bytes 1179652
  19.1 9.5 %copy-start.18 = (s32[4,6]{1,0:T(4,128)S(1)}, s32[4,6]{1,0:T(4,128)}, u32[]{:S(2)}) copy-start(s32[4,6]{1,0:T(4,128)} %param.21) | copy-start | bytes 292
  19.1 9.7 %copy-start.20 = (s32[4,6]{1,0:T(4,128)S(1)}, s32[4,6]{1,0:T(4,128)}, u32[]{:S(2)}) copy-start(s32[4,6]{1,0:T(4,128)} %param.22) | copy-start | bytes 292
  19.1 9.9 %slice-start.1 = ((bf16[4,64,4,3,64]{1,0,4,3,2:T(4,128)(2,1)}), bf16[4,64,4,1,64]{1,0,4,3,2:T(4,128)(2,1)S(1)}, s32[]{:S(2)}) async-start(bf16[4,64,4,3,64]{1,0,4,3,2:T(4,128)(2,1)} %reshape.174), calls=%async_computation.7 | async-start | bytes 524288 | tf_op jit(solution)/shard_map/slice | solution.py:66
  19.1 51.6 %all-to-all-start = ((bf16[16,2,64,512]{3,2,1,0:T(8,128)(2,1)}), bf16[16,2,64,512]{3,2,1,0:T(8,128)(2,1)}, u32[]{:S(2)}, u32[]{:S(2)}) async-start(bf16[16,2,64,512]{3,2,1,0:T(8,128)(2,1)} %bitcast.142), calls=%async_computation | async-start | bytes 4194304 | tf_op jit(solution)/shard_map/all_to_all | solution.py:79
  27.6 99.9 %all-reduce.17.cloned.1.call-start = ((), (), s32[]{:S(2)}) async-start(), calls=%async_computation.3 | async-start | bytes 1572864 | tf_op jit(solution)/shard_map/psum | solution.py:104
  29.2 60.4 %copy-start.12 = (bf16[4,64,4,1,64]{4,1,2,0,3:T(8,128)(2,1)}, bf16[4,64,4,1,64]{4,1,2,0,3:T(8,128)(2,1)S(1)}, u32[]{:S(2)}) copy-start(bf16[4,64,4,1,64]{4,1,2,0,3:T(8,128)(2,1)S(1)} %copy.61) | copy-start | bytes 393220
  81.2 8.5 %copy-start.10 = (bf16[4,64,4,2,64]{1,4,2,0,3:T(8,128)(2,1)S(1)}, bf16[4,64,4,2,64]{1,4,2,0,3:T(8,128)(2,1)}, u32[]{:S(2)}) copy-start(bf16[4,64,4,2,64]{1,4,2,0,3:T(8,128)(2,1)} %copy.60) | copy-start | bytes 786436
  93.2 5.2 %copy-start.11 = (bf16[256,768]{1,0:T(8,128)(2,1)S(1)}, bf16[256,768]{1,0:T(8,128)(2,1)}, u32[]{:S(2)}) copy-start(bf16[256,768]{1,0:T(8,128)(2,1)} %param.16) | copy-start | bytes 1179652
  99.6 27.9 %copy-start.1 = (bf16[4,64,768]{2,1,0:T(8,128)(2,1)S(1)}, bf16[4,64,768]{2,1,0:T(8,128)(2,1)}, u32[]{:S(2)}) copy-start(bf16[4,64,768]{2,1,0:T(8,128)(2,1)} %param.12) | copy-start | bytes 1179652
  138.8 2.3 copy-start.5
  138.8 2.8 copy-start.9
  138.8 2.8 copy-start.16
  142.7 1.4 copy-start.13
  188.6 7.1 %copy-start.19 = (s32[1,16,2]{1,2,0:T(2,128)S(1)}, s32[1,16,2]{1,2,0:T(2,128)}, u32[]{:S(2)}) copy-start(s32[1,16,2]{1,2,0:T(2,128)} %param.23) | copy-start | bytes 388
  188.6 50.4 %all-to-all-start.1 = ((bf16[16,2,64,512]{3,2,1,0:T(8,128)(2,1)}), bf16[16,2,64,512]{3,2,1,0:T(8,128)(2,1)}, u32[]{:S(2)}, u32[]{:S(2)}) async-start(bf16[16,2,64,512]{3,2,1,0:T(8,128)(2,1)} %bitcast.141), calls=%async_computation.1 | async-start | bytes 4194304 | tf_op jit(solution)/shard_map/all_to_all | solution.py:148
  195.7 83.9 %all-reduce.19.cloned.1.call-start = ((), (), s32[]{:S(2)}) async-start(), calls=%async_computation.4 | async-start | bytes 786432 | tf_op jit(solution)/shard_map/psum | solution.py:164
  195.9 43.1 %slice-start = ((f32[4,7,64,512]{3,2,1,0:T(8,128)}), f32[4,1,64,512]{3,2,1,0:T(8,128)S(1)}, s32[]{:S(2)}) async-start(f32[4,7,64,512]{3,2,1,0:T(8,128)} %reshape.181), calls=%async_computation.6 | async-start | bytes 1048576 | tf_op jit(solution)/shard_map/slice | solution.py:142
  250.9 5.3 %copy-start.4 = (bf16[4,64,768]{2,1,0:T(8,128)(2,1)S(1)}, bf16[4,64,768]{2,1,0:T(8,128)(2,1)}, u32[]{:S(2)}) copy-start(bf16[4,64,768]{2,1,0:T(8,128)(2,1)} %copy-done.3) | copy-start | bytes 1179652
  256.1 3.0 copy-start.15
  256.1 23.4 %copy-start.17 = (f32[768]{0:T(1024)S(1)}, f32[768]{0:T(1024)}, u32[]{:S(2)}) copy-start(f32[768]{0:T(1024)} %param.14) | copy-start | bytes 9220
  256.2 157.7 %reduce-scatter.2.cloned.1.call-start = ((), (), s32[]{:S(2)}) async-start(), calls=%async_computation.5 | async-start | bytes 2506752 | tf_op jit(solution)/shard_map/reduce_scatter | solution.py:169
  259.1 21.7 %copy-start.8 = (bf16[256,768]{1,0:T(8,128)(2,1)S(1)}, bf16[256,768]{1,0:T(8,128)(2,1)}, u32[]{:S(2)}) copy-start(bf16[256,768]{1,0:T(8,128)(2,1)} %copy-done.7) | copy-start | bytes 1179652
  (4 other events, 3.1 us)
Sparse Core Ops, SparseCore 0:
  103.9 23.5 all-reduce.16
  256.3 23.2 all-reduce.18
  285.0 128.7 reduce-scatter.1
where the time goes:
time: 422 us; the launch traced here: 420 us
  waiting for transfers between devices  254 us (60%)
  local copies, waits for them, and re-layouts  67 us (16%)
  matrix products  42.6 us (10%)
  other arithmetic  26.8 us (6%)
  starting transfers between devices  15.7 us (4%)
  between operations  14.1 us (3%)
    reduce_scatter x1, waiting for transfers between devices, body(): lax.psum_scatter(jnp.dot(hidden.T, grad_packed, preferred_element_type=jn...  131 us
    all_to_all x1, waiting for transfers between devices, body(): lax.all_to_all(returning.astype(jnp.bfloat16), 'tok', split_axis=0, conca...  40.7 us
    all_to_all x1, waiting for transfers between devices, body(): lax.all_to_all(outgoing, 'tok', split_axis=0, concat_axis=0, tiled=True)  39.2 us
    psum x1, waiting for transfers between devices, body(): total_out = lax.psum(partial_out, 'mdl')  23.7 us
    psum x1, waiting for transfers between devices, body(): lax.psum(grad_part.astype(jnp.bfloat16), 'mdl').astype(jnp.float32)  19.6 us
    reshape x2, local copies, waits for them, and re-layouts, body(): remote.reshape(own_bricks, face_count * per_brick, head_count, 2, head_size)  15.5 us
    another operation x1, local copies, waits for them, and re-layouts, body(): jnp.stack([grad_key, grad_value], axis=3)  11.9 us
    scatter-add x1, other arithmetic, body(): jnp.zeros((slot_total, per_brick, pair_width), jnp.float32).at[arrival]  9.63 us
  transfers between devices with their start and end apart: 5, of which 5 were waited for; matrix products, arithmetic and copies ran while one was open for 3% of the time, Pallas kernels for 0%

commit v1 on v0

v1 whole, which is shorter than its diff:
```python
import functools
import math

import jax
import jax.numpy as jnp
from jax import lax
from jax.experimental import pallas as pl
from jax.experimental.pallas import tpu as pltpu
from jax.sharding import PartitionSpec as P

fold_weight = 8.0
norm_eps = 1e-05
F32 = jnp.float32
BF16 = jnp.bfloat16
VM = pl.BlockSpec(memory_space=pltpu.VMEM)
SM = pl.BlockSpec(memory_space=pltpu.SMEM)
PARAMS = pltpu.CompilerParams(vmem_limit_bytes=40 << 20)


def dot_nn(a, b):
    return lax.dot_general(a, b, (((1,), (0,)), ((), ())), preferred_element_type=F32)


def dot_nt(a, b):
    return lax.dot_general(a, b, (((1,), (1,)), ((), ())), preferred_element_type=F32)


def dot_tn(a, b):
    return lax.dot_general(a, b, (((0,), (0,)), ((), ())), preferred_element_type=F32)


def gelu_tanh(value):
    return jax.nn.gelu(value, approximate=True)


def project_kernel(heads, dh, send, tok, gain, w, hidden, packed, outgoing, pairs):
    bricks, per, width = tok.shape
    x = tok[...].reshape(bricks * per, width).astype(F32)
    inv = lax.rsqrt(jnp.mean(x * x, axis=-1, keepdims=True) + norm_eps)
    h = (x * inv * gain[...]).astype(BF16)
    hidden[...] = h
    pk = dot_nn(h, w[...]).astype(BF16)
    packed[...] = pk
    for b in range(bricks):
        for n in range(heads):
            pairs[b, :, n * 2 * dh : (n + 1) * 2 * dh] = pk[
                b * per : (b + 1) * per, n * 3 * dh + dh : (n + 1) * 3 * dh
            ]

    def put(s, c):
        outgoing[s] = pairs[send[s]]
        return c

    lax.fori_loop(0, outgoing.shape[0], put, 0)


def fill_window(arrival, packed, incoming, window, b, heads, dh, per, faces):
    for n in range(heads):
        window[0:per, n * 2 * dh : (n + 1) * 2 * dh] = packed[
            b * per : (b + 1) * per, n * 3 * dh + dh : (n + 1) * 3 * dh
        ]
    for j in range(faces):
        window[(j + 1) * per : (j + 2) * per, :] = incoming[arrival[b * faces + j]]


def forward_kernel(heads, dh, per, faces, arrival, packed, incoming, bias, seen, attended, probs, window):
    bricks = packed.shape[0] // per
    scale = 1.0 / math.sqrt(dh)
    for b in range(bricks):
        fill_window(arrival, packed, incoming, window, b, heads, dh, per, faces)
        live = seen[b : b + 1, :] > 0
        rows = slice(b * per, (b + 1) * per)
        for n in range(heads):
            q = packed[rows, n * 3 * dh : n * 3 * dh + dh]
            k = window[:, n * 2 * dh : n * 2 * dh + dh]
            v = window[:, n * 2 * dh + dh : (n + 1) * 2 * dh]
            s = dot_nt(q, k) * scale + bias[n]
            s = jnp.where(live, s, -1000000000.0)
            e = jnp.exp(s - jnp.max(s, axis=-1, keepdims=True))
            p = e * (1.0 / jnp.sum(e, axis=-1, keepdims=True))
            probs[b * heads + n] = p
            attended[rows, n * dh : (n + 1) * dh] = dot_nn(p.astype(BF16), v).astype(BF16)


def backward_kernel(
    heads, dh, per, faces, arrival, packed, incoming, probs, mixed, gquery, gown, returning, window, gwin
):
    bricks = packed.shape[0] // per
    scale = 1.0 / math.sqrt(dh)

    def clear(s, c):
        returning[s] = jnp.zeros(returning.shape[1:], BF16)
        return c

    lax.fori_loop(0, returning.shape[0], clear, 0)
    for b in range(bricks):
        fill_window(arrival, packed, incoming, window, b, heads, dh, per, faces)
        rows = slice(b * per, (b + 1) * per)
        for n in range(heads):
            q = packed[rows, n * 3 * dh : n * 3 * dh + dh]
            k = window[:, n * 2 * dh : n * 2 * dh + dh]
            v = window[:, n * 2 * dh + dh : (n + 1) * 2 * dh]
            p = probs[b * heads + n]
            g = mixed[rows, n * dh : (n + 1) * dh]
            dp = dot_nt(g, v)
            ds = p * (dp - jnp.sum(p * dp, axis=-1, keepdims=True))
            low = ds.astype(BF16)
            gquery[rows, n * dh : (n + 1) * dh] = dot_nn(low, k) * scale
            gwin[:, n * 2 * dh : n * 2 * dh + dh] = dot_tn(low, q) * scale
            gwin[:, n * 2 * dh + dh : (n + 1) * 2 * dh] = dot_tn(p.astype(BF16), g)
        gown[b] = gwin[0:per, :]
        for j in range(faces):
            returning[arrival[b * faces + j]] = gwin[(j + 1) * per : (j + 2) * per, :].astype(BF16)


def collect_kernel(heads, dh, send, returned, gquery, gown, gpacked, acc):
    bricks, per, _ = gown.shape
    acc[...] = gown[...]

    def add(s, c):
        acc[send[s]] += returned[s].astype(F32)
        return c

    lax.fori_loop(0, returned.shape[0], add, 0)
    for b in range(bricks):
        rows = slice(b * per, (b + 1) * per)
        for n in range(heads):
            gpacked[rows, n * 3 * dh : n * 3 * dh + dh] = gquery[rows, n * dh : (n + 1) * dh].astype(BF16)
            gpacked[rows, n * 3 * dh + dh : (n + 1) * 3 * dh] = acc[
                b, :, n * 2 * dh : (n + 1) * 2 * dh
            ].astype(BF16)


def swap(src, dst, send_sem, recv_sem):
    other = 1 - lax.axis_index("mdl")
    barrier = pltpu.get_barrier_semaphore()
    pl.semaphore_signal(barrier, inc=1, device_id={"mdl": other}, device_id_type=pl.DeviceIdType.MESH)
    pl.semaphore_wait(barrier, 1)
    copy = pltpu.make_async_remote_copy(
        src_ref=src,
        dst_ref=dst,
        send_sem=send_sem,
        recv_sem=recv_sem,
        device_id={"mdl": other},
        device_id_type=pl.DeviceIdType.MESH,
    )
    copy.start()
    return copy


def fold_math(x, total, cot, w_disp, folding, grad_out):
    out = (x.astype(F32) + total).astype(BF16)
    disp = lax.dot_general(w_disp, out, (((0,), (1,)), ((), ())), preferred_element_type=F32)
    vox = disp.shape[0] // 3
    steps = (1, 4, 16)
    comp = [disp[c * vox : (c + 1) * vox] for c in range(3)]
    row = lax.broadcasted_iota(jnp.int32, comp[0].shape, 0)
    inside = ((row & 3) < 3) & (((row >> 2) & 3) < 3) & ((row >> 4) < 3)
    jac = [
        [
            pltpu.roll(comp[i], vox - steps[k], 0) - comp[i] + (1.0 if i == k else 0.0)
            for k in range(3)
        ]
        for i in range(3)
    ]
    cof = [[None] * 3 for _ in range(3)]
    for i in range(3):
        i1, i2 = (i + 1) % 3, (i + 2) % 3
        for k in range(3):
            k1, k2 = (k + 1) % 3, (k + 2) % 3
            cof[i][k] = jac[i1][k1] * jac[i2][k2] - jac[i1][k2] * jac[i2][k1]
    det = jac[0][0] * cof[0][0] + jac[0][1] * cof[0][1] + jac[0][2] * cof[0][2]
    small = jnp.exp(-jnp.abs(det))
    soft = jnp.maximum(-det, 0.0) + jnp.log1p(small)
    folding[...] = jnp.sum(jnp.where(inside, soft, 0.0), axis=0, keepdims=True) * (1.0 / 27.0)
    sig = jnp.where(det > 0, small, 1.0) / (1.0 + small)
    coef = jnp.where(inside, sig * (-fold_weight / 27.0), 0.0)
    grads = []
    for i in range(3):
        g = jnp.zeros_like(det)
        for k in range(3):
            t = jnp.where(inside, coef * cof[i][k], 0.0)
            g = g + pltpu.roll(t, steps[k], 0) - t
        grads.append(g)
    gd = jnp.concatenate(grads, axis=0).astype(BF16)
    back = lax.dot_general(gd, w_disp, (((0,), (1,)), ((), ())), preferred_element_type=F32)
    grad_out[...] = (cot.astype(F32) + back).astype(BF16)


def fold_swap_kernel(x, part, cot, w_disp, folding, grad_out, other, send_sem, recv_sem):
    swap(part, other, send_sem, recv_sem).wait()
    fold_math(x[...], part[...] + other[...], cot[...], w_disp[...], folding, grad_out)


def fold_kernel(x, part, cot, w_disp, folding, grad_out):
    fold_math(x[...], part[...], cot[...], w_disp[...], folding, grad_out)


def norm_math(x, grad_hidden, grad_out, gain, out):
    x = x.astype(F32)
    inv = lax.rsqrt(jnp.mean(x * x, axis=-1, keepdims=True) + norm_eps)
    normed = x * inv
    g = grad_hidden * gain
    out[...] = (
        grad_out.astype(F32) + inv * (g - normed * jnp.mean(g * normed, axis=-1, keepdims=True))
    ).astype(BF16)


def norm_swap_kernel(x, part, grad_out, gain, out, other, send_sem, recv_sem):
    swap(part, other, send_sem, recv_sem).wait()
    norm_math(x[...], part[...].astype(F32) + other[...].astype(F32), grad_out[...], gain[...], out)


def norm_kernel(x, part, grad_out, gain, out):
    norm_math(x[...], part[...].astype(F32), grad_out[...], gain[...], out)


def body(
    tokens,
    cotangent,
    norm_gain,
    w_qkv,
    w_out,
    w_up,
    w_down,
    w_disp,
    rel_bias,
    face_source,
    face_live,
    send_bricks,
):
    bricks, per, width = tokens.shape
    rows = bricks * per
    heads = rel_bias.shape[0]
    dh = w_out.shape[0] // heads
    faces = face_source.shape[1]
    devices = lax.axis_size("tok")
    pair = lax.axis_size("mdl") == 2
    slots = send_bricks.shape[2]
    total = devices * slots
    kv = heads * 2 * dh
    span = (faces + 1) * per
    send = send_bricks.reshape(-1)
    sources = face_source.reshape(-1)
    matches = (sources[:, None] == sources[None, :]).astype(jnp.int32)
    count = sources.shape[0]
    before = jnp.arange(count)[None, :] < jnp.arange(count)[:, None]
    arrival = sources * slots + jnp.sum(jnp.where(before, matches, 0), axis=1)
    seen = jnp.concatenate([jnp.ones((bricks, 1), jnp.int32), face_live], axis=1)
    seen = jnp.repeat(seen, per, axis=1)
    gain = norm_gain.reshape(1, width)
    flat = tokens.reshape(rows, width)

    hidden, packed, outgoing = pl.pallas_call(
        functools.partial(project_kernel, heads, dh),
        out_shape=(
            jax.ShapeDtypeStruct((rows, width), BF16),
            jax.ShapeDtypeStruct((rows, heads * 3 * dh), BF16),
            jax.ShapeDtypeStruct((total, per, kv), BF16),
        ),
        in_specs=[SM, VM, VM, VM],
        out_specs=(VM, VM, VM),
        scratch_shapes=[pltpu.VMEM((bricks, per, kv), BF16)],
        compiler_params=PARAMS,
        name="project",
    )(send, tokens, gain, w_qkv)

    incoming = lax.all_to_all(outgoing, "tok", split_axis=0, concat_axis=0, tiled=True)

    up_pre = jnp.dot(hidden, w_up, preferred_element_type=F32)
    activ, gelu_back = jax.vjp(gelu_tanh, up_pre)
    part_ffn = jnp.dot(activ.astype(BF16), w_down, preferred_element_type=F32)

    attended, probs = pl.pallas_call(
        functools.partial(forward_kernel, heads, dh, per, faces),
        out_shape=(
            jax.ShapeDtypeStruct((rows, heads * dh), BF16),
            jax.ShapeDtypeStruct((bricks * heads, per, span), F32),
        ),
        in_specs=[SM, VM, VM, VM, VM],
        out_specs=(VM, VM),
        scratch_shapes=[pltpu.VMEM((span, kv), BF16)],
        compiler_params=PARAMS,
        name="attend",
    )(arrival, packed, incoming, rel_bias, seen)

    part_out = part_ffn + jnp.dot(attended, w_out, preferred_element_type=F32)
    fold_shape = (
        jax.ShapeDtypeStruct((1, rows), F32),
        jax.ShapeDtypeStruct((rows, width), BF16),
    )
    cot = cotangent.reshape(rows, width)
    if pair:
        folding, grad_out = pl.pallas_call(
            fold_swap_kernel,
            out_shape=fold_shape,
            in_specs=[VM] * 4,
            out_specs=(VM, VM),
            scratch_shapes=[
                pltpu.VMEM((rows, width), F32),
                pltpu.SemaphoreType.DMA,
                pltpu.SemaphoreType.DMA,
            ],
            compiler_params=pltpu.CompilerParams(
                vmem_limit_bytes=40 << 20, collective_id=0, has_side_effects=True
            ),
            name="fold_swap",
        )(flat, part_out, cot, w_disp)
    else:
        folding, grad_out = pl.pallas_call(
            fold_kernel,
            out_shape=fold_shape,
            in_specs=[VM] * 4,
            out_specs=(VM, VM),
            compiler_params=PARAMS,
            name="fold",
        )(flat, lax.psum(part_out, "mdl"), cot, w_disp)

    grad_mixed = jnp.dot(grad_out, w_out.T, preferred_element_type=F32).astype(BF16)

    gquery, gown, returning = pl.pallas_call(
        functools.partial(backward_kernel, heads, dh, per, faces),
        out_shape=(
            jax.ShapeDtypeStruct((rows, heads * dh), F32),
            jax.ShapeDtypeStruct((bricks, per, kv), F32),
            jax.ShapeDtypeStruct((total, per, kv), BF16),
        ),
        in_specs=[SM, VM, VM, VM, VM],
        out_specs=(VM, VM, VM),
        scratch_shapes=[pltpu.VMEM((span, kv), BF16), pltpu.VMEM((span, kv), F32)],
        compiler_params=PARAMS,
        name="attend_back",
    )(arrival, packed, incoming, probs, grad_mixed)

    returned = lax.all_to_all(returning, "tok", split_axis=0, concat_axis=0, tiled=True)

    grad_act = jnp.dot(grad_out, w_down.T, preferred_element_type=F32)
    grad_pre = gelu_back(grad_act)[0].astype(BF16)
    part_up = jnp.dot(grad_pre, w_up.T, preferred_element_type=F32)

    grad_packed = pl.pallas_call(
        functools.partial(collect_kernel, heads, dh),
        out_shape=jax.ShapeDtypeStruct((rows, heads * 3 * dh), BF16),
        in_specs=[SM, VM, VM, VM],
        out_specs=VM,
        scratch_shapes=[pltpu.VMEM((bricks, per, kv), F32)],
        compiler_params=PARAMS,
        name="collect",
    )(send, returned, gquery, gown)

    terms = lax.dot_general(
        hidden, grad_packed, (((0,), (0,)), ((), ())), preferred_element_type=F32
    ).astype(BF16)
    terms = terms.reshape(devices, width // devices, heads * 3 * dh)
    terms = lax.all_to_all(terms, "tok", split_axis=0, concat_axis=0, tiled=True)
    grad_weight = jnp.sum(terms.astype(F32), axis=0)

    grad_part = (part_up + jnp.dot(grad_packed, w_qkv.T, preferred_element_type=F32)).astype(BF16)
    norm_shape = jax.ShapeDtypeStruct((rows, width), BF16)
    if pair:
        grad_tokens = pl.pallas_call(
            norm_swap_kernel,
            out_shape=norm_shape,
            in_specs=[VM] * 4,
            out_specs=VM,
            scratch_shapes=[
                pltpu.VMEM((rows, width), BF16),
                pltpu.SemaphoreType.DMA,
                pltpu.SemaphoreType.DMA,
            ],
            compiler_params=pltpu.CompilerParams(
                vmem_limit_bytes=40 << 20, collective_id=1, has_side_effects=True
            ),
            name="norm_swap",
        )(flat, grad_part, grad_out, gain)
    else:
        grad_tokens = pl.pallas_call(
            norm_kernel,
            out_shape=norm_shape,
            in_specs=[VM] * 4,
            out_specs=VM,
            compiler_params=PARAMS,
            name="norm",
        )(flat, lax.psum(grad_part, "mdl"), grad_out, gain)
    return (folding.reshape(bricks, per), grad_tokens.reshape(bricks, per, width), grad_weight)


def solution(mesh):
    return jax.shard_map(
        body,
        mesh=mesh,
        in_specs=(
            P("tok", None, None),
            P("tok", None, None),
            P(),
            P(None, "mdl"),
            P("mdl", None),
            P(None, "mdl"),
            P("mdl", None),
            P(),
            P("mdl", None, None),
            P("tok", None),
            P("tok", None),
            P("tok", None, None),
        ),
        out_specs=(P("tok", None), P("tok", None, None), P("tok", "mdl")),
        check_vma=False,
    )
```

time: 422 us -> 180 us (0.43)
  waiting for transfers between devices: 254 us -> 50 us
  blocking collectives: 0 us -> 58.9 us
  local copies, waits for them, and re-layouts: 67 us -> 14.1 us
  matrix products: 42.6 us -> 11.8 us
  Pallas kernels: 0 us -> 25.6 us
  other arithmetic: 26.8 us -> 4.85 us
  between operations: 14.1 us -> 0.85 us
    reduce_scatter x1 -> x0, waiting for transfers between devices: 131 us -> none  [body(): lax.psum_scatter(jnp.dot(hidden.T, grad_packed, preferred_element_type=jn...]
    all_to_all x0 -> x1, blocking collectives: none -> 58.9 us  [body(): lax.all_to_all(returning, 'tok', split_axis=0, concat_axis=0, tiled=True)]
    psum x2 -> x0, waiting for transfers between devices: 43.4 us -> none  [the longest x1 23.7 us: body(): total_out = lax.psum(partial_out, 'mdl')]
    reshape x10 -> x5, local copies, waits for them, and re-layouts: 31.7 us -> 2.26 us  [the longest x1 0.84 us: body(): gain = norm_gain.reshape(1, width)]
    dot_general x16 -> x7, matrix products: 39 us -> 11.8 us  [the longest x1 5.17 us: body(): part_up = jnp.dot(grad_pre, w_up.T, preferred_element_type=F32)]
    all_to_all x1, waiting for transfers between devices: 40.7 us -> 14.9 us  [body(): lax.all_to_all(terms, 'tok', split_axis=0, concat_axis=0, tiled=True)]
    pallas_call x0 -> x6, Pallas kernels: none -> 25.6 us  [the longest x1 9.38 us: body(): pl.pallas_call(functools.partial(backward_kernel, heads, dh, per, faces),...]
    another operation x1 -> x0, local copies, waits for them, and re-layouts: 11.9 us -> none  [body(): jnp.stack([grad_key, grad_value], axis=3)]
  transfers between devices with their start and end apart: 5 -> 2, of which waited for: 5 -> 2; matrix products, arithmetic and copies ran while one was open for 3% -> 9% of each run, Pallas kernels for 0% -> 1%
where the time goes in v1:
time: 180 us; the launch traced here: 179 us
  blocking collectives  58.9 us (33%)
  waiting for transfers between devices  50 us (28%)
  Pallas kernels  25.6 us (14%)
  local copies, waits for them, and re-layouts  14.1 us (8%)
  starting transfers between devices  12.9 us (7%)
  matrix products  11.8 us (7%)
  other arithmetic  4.85 us (3%)
    all_to_all x1, blocking collectives, body(): lax.all_to_all(returning, 'tok', split_axis=0, concat_axis=0, tiled=True)  58.9 us
    all_to_all x1, waiting for transfers between devices, body(): lax.all_to_all(outgoing, 'tok', split_axis=0, concat_axis=0, tiled=True)  35.1 us
    all_to_all x1, waiting for transfers between devices, body(): lax.all_to_all(terms, 'tok', split_axis=0, concat_axis=0, tiled=True)  14.9 us
    unnamed x43, local copies, waits for them, and re-layouts  11.1 us
    pallas_call x1, Pallas kernels, body(): pl.pallas_call(functools.partial(backward_kernel, heads, dh, per, faces),...  9.38 us
    all_to_all x1, starting transfers between devices, body(): lax.all_to_all(outgoing, 'tok', split_axis=0, concat_axis=0, tiled=True)  8.49 us
    pallas_call x1, Pallas kernels, body(): pl.pallas_call(functools.partial(forward_kernel, heads, dh, per, faces),...  8.17 us
    dot_general x1, matrix products, body(): part_up = jnp.dot(grad_pre, w_up.T, preferred_element_type=F32)  5.17 us
  transfers between devices with their start and end apart: 2, of which 2 were waited for; matrix products, arithmetic and copies ran while one was open for 9% of the time, Pallas kernels for 1%

profile of v1, /device:TPU:0, one launch (start us, length us, event | category | flops | bytes accessed | tf_op | source)
XLA Modules:
  0.0 178.9 jit_solution(10098226641583837250)
XLA Ops:
  2.3 1.3 copy-done.1
  3.6 1.0 copy-done.3
  4.6 1.4 project.1
  6.1 1.3 copy-done.7
  7.4 8.5 %all-to-all-start = ((bf16[32,64,512]{2,1,0:T(8,128)(2,1)}), bf16[32,64,512]{2,1,0:T(8,128)(2,1)}, u32[]{:S(2)}, u32[]{:S(2)}) async-start(bf16[32,64,512]{2,1,0:T(8,128)(2,1)} %copy-done.7), calls=%async_computation | async-start | bytes 4194304 | tf_op jit(solution)/shard_map/all_to_all | solution.py:268
  16.7 1.1 copy.20.w_disp
  17.8 0.9 select_reduce_fusion
  18.8 1.2 multiply_add_fusion.arrival
  20.7 1.2 copy-done.15
  21.9 1.9 %fusion.8 = f32[256,768]{1,0:T(8,128)} fusion(bf16[1536,768]{1,0:T(8,128)(2,1)S(1)} %copy-done.19, f32[256,1536]{1,0:T(8,128)S(1)} %fusion.27), kind=kOutput, calls=%fused_computation.16 | convolution fusion | flops 607518720 | bytes 4718592 | tf_op jit(solution)/shard_map/dot_general | solution.py:272
  23.9 35.1 %all-to-all-done.incoming = bf16[32,64,512]{2,1,0:T(8,128)(2,1)} async-done(((bf16[32,64,512]{2,1,0:T(8,128)(2,1)}), bf16[32,64,512]{2,1,0:T(8,128)(2,1)}, u32[]{:S(2)}, u32[]{:S(2)}) %all-to-all-start) | async-done | bytes 2097184 | tf_op jit(solution)/shard_map/all_to_all | solution.py:268
  59.0 1.0 copy-done.10
  60.7 8.2 %attend.1 = (bf16[256,256]{1,0:T(8,128)(2,1)S(1)}, f32[16,64,448]{2,1,0:T(8,128)S(1)}) custom-call(s32[24]{0:T(128)S(1)} %copy-done.12, bf16[256,768]{1,0:T(8,128)(2,1)S(1)} %get-tuple-element.14.packed, bf16[32,64,512]{2,1,0:T(8,128)(2,1)} %all-to-all-done.incoming, f32[4,64,448]{2,1,0:T(8,128)S(1)} %copy-done.10, s32[4,448]{1,0:T(4,128)S(1)} %reshape.39.seen), custom_call_target="tpu_custom_call" | custom-call | tf_op jit(solution)/shard_map/attend/pallas_call | solution.py:274
  70.0 3.3 %fold_swap.1 = (f32[1,256]{1,0:T(1,128)S(1)}, bf16[256,768]{1,0:T(8,128)(2,1)S(1)}) custom-call(bf16[256,768]{1,0:T(8,128)(2,1)S(1)} %bitcast.18, f32[256,768]{1,0:T(8,128)S(1)} %convolution_add_fusion.1.part, bf16[256,768]{1,0:T(8,128)(2,1)S(1)} %bitcast.21, bf16[768,192]{1,0:T(8,128)(2,1)S(1)} %copy.20.w_disp), custom_call_target="tpu_custom_call" | custom-call | tf_op jit(solution)/shard_map/fold_swap/pallas_call | solution.py:294
  74.0 9.4 %attend_back.1 = (f32[256,256]{1,0:T(8,128)S(1)}, f32[4,64,512]{2,1,0:T(8,128)S(1)}, bf16[32,64,512]{2,1,0:T(8,128)(2,1)S(1)}) custom-call(s32[24]{0:T(128)S(1)} %copy-done.13, bf16[256,768]{1,0:T(8,128)(2,1)S(1)} %get-tuple-element.14.packed, bf16[32,64,512]{2,1,0:T(8,128)(2,1)} %all-to-all-done.incoming, f32[16,64,448]{2,1,0:T(8,128)S(1)} %get-tuple-element.19.probs, ...), custom_call_target="tpu_custom_call" | custom-call | tf_op jit(solution)/shard_map/attend_back/pallas_call | solution.py:321
  83.4 58.9 %all_to_all.15.returned = bf16[32,64,512]{2,1,0:T(8,128)(2,1)S(1)} all-to-all(bf16[32,64,512]{2,1,0:T(8,128)(2,1)S(1)} %get-tuple-element.20), channel_id=1, replica_groups=mesh['tok'=16,'mdl'=2] {'tok'}, dimensions={0} | all-to-all | bytes 4194304 | tf_op jit(solution)/shard_map/all_to_all | solution.py:335
  142.3 1.2 collect.1
  144.3 1.5 convolution_convert_fusion
  145.8 4.4 %all-to-all-start.2 = ((bf16[16,48,768]{2,1,0:T(8,128)(2,1)}), bf16[16,48,768]{2,1,0:T(8,128)(2,1)}, u32[]{:S(2)}, u32[]{:S(2)}) async-start(bf16[16,48,768]{2,1,0:T(8,128)(2,1)} %bitcast.22), calls=%async_computation.2 | async-start | bytes 2359296 | tf_op jit(solution)/shard_map/all_to_all | solution.py:355
  152.0 5.2 %fusion.13 = f32[256,768]{1,0:T(8,128)} fusion(bf16[768,1536]{1,0:T(8,128)(2,1)S(1)} %copy-done, f32[256,1536]{1,0:T(8,128)} %copy-done.15, bf16[256,768]{1,0:T(8,128)(2,1)} %copy-done.8, bf16[1536,768]{1,0:T(8,128)(2,1)} %param.18), kind=kOutput, calls=%fused_computation.21 | convolution fusion | flops 1215823872 | bytes 7471104 | tf_op jit(solution)/shard_map/dot_general | solution.py:339
  157.2 1.8 %fusion.7.part = bf16[256,768]{1,0:T(8,128)(2,1)S(1)} fusion(f32[256,768]{1,0:T(8,128)} %fusion.13, bf16[256,768]{1,0:T(8,128)(2,1)} %copy-done.6, bf16[768,768]{1,0:T(8,128)(2,1)S(1)} %copy-done.2), kind=kOutput, calls=%fused_computation.14 | convolution fusion | flops 302383104 | bytes 2752512 | tf_op jit(solution)/shard_map/dot_general | solution.py:358
  159.0 2.2 %norm_swap.1 = bf16[256,768]{1,0:T(8,128)(2,1)S(1)} custom-call(bf16[256,768]{1,0:T(8,128)(2,1)S(1)} %bitcast.19, bf16[256,768]{1,0:T(8,128)(2,1)S(1)} %fusion.7.part, bf16[256,768]{1,0:T(8,128)(2,1)S(1)} %copy-done.9, f32[1,768]{1,0:T(1,128)S(1)} %reshape.37.gain), custom_call_target="tpu_custom_call" | custom-call | tf_op jit(solution)/shard_map/norm_swap/pallas_call | solution.py:361
  161.2 14.9 %all-to-all-done.2 = bf16[16,48,768]{2,1,0:T(8,128)(2,1)} async-done(((bf16[16,48,768]{2,1,0:T(8,128)(2,1)}), bf16[16,48,768]{2,1,0:T(8,128)(2,1)}, u32[]{:S(2)}, u32[]{:S(2)}) %all-to-all-start.2) | async-done | bytes 1179680 | tf_op jit(solution)/shard_map/all_to_all | solution.py:355
  176.1 2.1 %convert_reduce_fusion = f32[48,768]{1,0:T(8,128)} fusion(bf16[16,48,768]{2,1,0:T(8,128)(2,1)} %all-to-all-done.2), kind=kLoop, calls=%fused_computation | loop fusion | flops 1142784 | bytes 1327104 | tf_op jit(solution)/shard_map/reduce_sum | solution.py:356
  (49 shorter events, 9.1 us)
Async XLA Ops:
  0.6 19.3 %copy-start = (bf16[768,1536]{1,0:T(8,128)(2,1)S(1)}, bf16[768,1536]{1,0:T(8,128)(2,1)}, u32[]{:S(2)}) copy-start(bf16[768,1536]{1,0:T(8,128)(2,1)} %param.17) | copy-start | bytes 7077892
  2.3 1.3 copy-start.1
  3.6 1.0 copy-start.3
  6.0 1.3 copy-start.7
  7.4 8.5 %copy-start.17 = (s32[4,6]{1,0:T(4,128)S(1)}, s32[4,6]{1,0:T(4,128)}, u32[]{:S(2)}) copy-start(s32[4,6]{1,0:T(4,128)} %param.21) | copy-start | bytes 292
  7.4 9.1 %copy-start.18 = (s32[4,6]{1,0:T(4,128)S(1)}, s32[4,6]{1,0:T(4,128)}, u32[]{:S(2)}) copy-start(s32[4,6]{1,0:T(4,128)} %param.22) | copy-start | bytes 292
  7.4 51.6 %all-to-all-start = ((bf16[32,64,512]{2,1,0:T(8,128)(2,1)}), bf16[32,64,512]{2,1,0:T(8,128)(2,1)}, u32[]{:S(2)}, u32[]{:S(2)}) async-start(bf16[32,64,512]{2,1,0:T(8,128)(2,1)} %copy-done.7), calls=%async_computation | async-start | bytes 4194304 | tf_op jit(solution)/shard_map/all_to_all | solution.py:268
  19.9 2.0 %copy-start.19 = (bf16[1536,768]{1,0:T(8,128)(2,1)S(1)}, bf16[1536,768]{1,0:T(8,128)(2,1)}, u32[]{:S(2)}) copy-start(bf16[1536,768]{1,0:T(8,128)(2,1)} %param.18) | copy-start | bytes 7077892
  20.7 1.2 copy-start.15
  59.0 1.0 copy-start.10
  60.0 0.7 copy-start.12
  60.7 8.2 %copy-start.14 = (bf16[256,768]{1,0:T(8,128)(2,1)S(1)}, bf16[256,768]{1,0:T(8,128)(2,1)}, u32[]{:S(2)}) copy-start(bf16[256,768]{1,0:T(8,128)(2,1)} %param.16) | copy-start | bytes 1179652
  60.7 8.2 %copy-start.16 = (f32[256,768]{1,0:T(8,128)S(1)}, f32[256,768]{1,0:T(8,128)}, u32[]{:S(2)}) copy-start(f32[256,768]{1,0:T(8,128)} %fusion.8) | copy-start | bytes 2359300
  68.9 1.0 copy-start.4
  68.9 1.1 copy-start.11
  69.2 4.8 %copy-start.13 = (s32[24]{0:T(128)S(1)}, s32[24]{0:T(128)}, u32[]{:S(2)}) copy-start(s32[24]{0:T(128)} %multiply_add_fusion.arrival) | copy-start | bytes 292
  73.3 0.7 copy-start.8
  143.5 0.8 copy-start.6
  145.8 30.3 %all-to-all-start.2 = ((bf16[16,48,768]{2,1,0:T(8,128)(2,1)}), bf16[16,48,768]{2,1,0:T(8,128)(2,1)}, u32[]{:S(2)}, u32[]{:S(2)}) async-start(bf16[16,48,768]{2,1,0:T(8,128)(2,1)} %bitcast.22), calls=%async_computation.2 | async-start | bytes 2359296 | tf_op jit(solution)/shard_map/all_to_all | solution.py:355
  152.0 5.2 %copy-start.2 = (bf16[768,768]{1,0:T(8,128)(2,1)S(1)}, bf16[768,768]{1,0:T(8,128)(2,1)}, u32[]{:S(2)}) copy-start(bf16[768,768]{1,0:T(8,128)(2,1)} %w.1) | copy-start | bytes 3538948
  157.2 1.8 %copy-start.5 = (bf16[4,64,768]{2,1,0:T(8,128)(2,1)S(1)}, bf16[4,64,768]{2,1,0:T(8,128)(2,1)}, u32[]{:S(2)}) copy-start(bf16[4,64,768]{2,1,0:T(8,128)(2,1)} %tok.1) | copy-start | bytes 1179652
  157.2 1.8 %copy-start.9 = (bf16[256,768]{1,0:T(8,128)(2,1)S(1)}, bf16[256,768]{1,0:T(8,128)(2,1)}, u32[]{:S(2)}) copy-start(bf16[256,768]{1,0:T(8,128)(2,1)} %copy-done.8) | copy-start | bytes 1179652

commit v2 on v1

--- a/solution.py
+++ b/solution.py
@@ -215,7 +215,7 @@
     norm_math(x[...], part[...].astype(F32), grad_out[...], gain[...], out)
 
 
-def body(
+def body_wide(
     tokens,
     cotangent,
     norm_gain,
@@ -385,9 +385,477 @@
     return (folding.reshape(bricks, per), grad_tokens.reshape(bricks, per, width), grad_weight)
 
 
+def gelu_slope(u):
+    c = math.sqrt(2.0 / math.pi)
+    t = jnp.tanh(c * (u + 0.044715 * (u * u * u)))
+    return 0.5 * (1.0 + t) + 0.5 * u * (1.0 - t * t) * c * (1.0 + (3.0 * 0.044715) * (u * u))
+
+
+def remote(src, dst, send_sem, recv_sem, where):
+    return pltpu.make_async_remote_copy(
+        src_ref=src,
+        dst_ref=dst,
+        send_sem=send_sem,
+        recv_sem=recv_sem,
+        device_id=where,
+        device_id_type=pl.DeviceIdType.MESH,
+    )
+
+
+def greet(me, count, other):
+    barrier = pltpu.get_barrier_semaphore()
+
+    def hail(i, c):
+        peer = lax.rem(me + i + 1, count)
+        pl.semaphore_signal(barrier, inc=1, device_id={"tok": peer}, device_id_type=pl.DeviceIdType.MESH)
+        return c
+
+    lax.fori_loop(0, count - 1, hail, 0)
+    pl.semaphore_signal(barrier, inc=1, device_id={"mdl": other}, device_id_type=pl.DeviceIdType.MESH)
+    pl.semaphore_wait(barrier, count)
+
+
+def gather_kernel(
+    count, send, tok, gain, wq_hbm, wup_hbm, wdn_hbm,
+    recv, hidden, packed, up_pre, part,
+    msg, wq, wup, wdn, wsem, ssem, rsem, fssem, frsem,
+):
+    me, core = lax.axis_index("tok"), lax.axis_index("mdl")
+    other = 1 - core
+    bricks, per, width = tok.shape
+    slots = recv.shape[1]
+    half = per // 2
+    mine = pl.ds(pl.multiple_of(core * half, half), half)
+    theirs = pl.ds(pl.multiple_of(other * half, half), half)
+    loads = [
+        pltpu.make_async_copy(a, b, wsem.at[i])
+        for i, (a, b) in enumerate(((wq_hbm, wq), (wup_hbm, wup), (wdn_hbm, wdn)))
+    ]
+    for load in loads:
+        load.start()
+    greet(me, count, other)
+
+    def out_copy(i):
+        peer = lax.rem(me + i + 1, count)
+        return remote(msg.at[i], recv.at[me, :, mine, :], ssem.at[i], rsem.at[i], {"tok": peer})
+
+    def launch(i, c):
+        peer = lax.rem(me + i + 1, count)
+        for k in range(slots):
+            msg[i, k] = tok[send[peer * slots + k], mine, :]
+        out_copy(i).start()
+        return c
+
+    lax.fori_loop(0, count - 1, launch, 0)
+    for k in range(slots):
+        recv[me, k] = tok[send[me * slots + k]]
+    x = tok[...].reshape(bricks * per, width).astype(F32)
+    inv = lax.rsqrt(jnp.mean(x * x, axis=-1, keepdims=True) + norm_eps)
+    hidden[...] = (x * inv * gain[...]).astype(BF16)
+    loads[0].wait()
+    packed[...] = dot_nn(hidden[...], wq[...]).astype(BF16)
+    loads[1].wait()
+    loads[2].wait()
+    ff = wup.shape[1]
+    step = ff // 3
+    for n in range(3):
+        cols = slice(n * step, (n + 1) * step)
+        u = dot_nn(hidden[...], wup[:, cols])
+        up_pre[:, cols] = u
+        term = dot_nn(gelu_tanh(u).astype(BF16), wdn[cols, :])
+        part[...] = term if n == 0 else part[...] + term
+
+    def relay_copy(i, rows):
+        source = lax.rem(me - (i + 1) + count, count)
+        block = recv.at[source, :, rows, :]
+        return remote(block, block, fssem.at[i], frsem.at[i], {"mdl": other})
+
+    def relay(i, c):
+        source = lax.rem(me - (i + 1) + count, count)
+        remote(msg.at[i], recv.at[source, :, mine, :], ssem.at[i], rsem.at[i], {"tok": source}).wait_recv()
+        relay_copy(i, mine).start()
+        return c
+
+    lax.fori_loop(0, count - 1, relay, 0)
+
+    def finish(i, c):
+        out_copy(i).wait_send()
+        relay_copy(i, mine).wait_send()
+        relay_copy(i, theirs).wait_recv()
+        return c
+
+    lax.fori_loop(0, count - 1, finish, 0)
+
+
+def attend_kernel(
+    heads, dh, per, faces, arrival, hidden, packed, recv, gain, wq, bias, seen,
+    attended, probs, window, hid, near,
+):
+    bricks = packed.shape[0] // per
+    scale = 1.0 / math.sqrt(dh)
+    for b in range(bricks):
+        rows = slice(b * per, (b + 1) * per)
+        for j in range(faces):
+            near[j * per : (j + 1) * per, :] = recv[arrival[b * faces + j]]
+        x = near[...].astype(F32)
+        inv = lax.rsqrt(jnp.mean(x * x, axis=-1, keepdims=True) + norm_eps)
+        h = (x * inv * gain[...]).astype(BF16)
+        hid[b, 0:per, :] = hidden[rows, :]
+        hid[b, per:, :] = h
+        pk = dot_nn(h, wq[...]).astype(BF16)
+        for n in range(heads):
+            two = slice(n * 2 * dh, (n + 1) * 2 * dh)
+            window[b, 0:per, two] = packed[rows, n * 3 * dh + dh : (n + 1) * 3 * dh]
+            window[b, per:, two] = pk[:, n * 3 * dh + dh : (n + 1) * 3 * dh]
+        live = seen[b : b + 1, :] > 0
+        for n in range(heads):
+            q = packed[rows, n * 3 * dh : n * 3 * dh + dh]
+            k = window[b, :, n * 2 * dh : n * 2 * dh + dh]
+            v = window[b, :, n * 2 * dh + dh : (n + 1) * 2 * dh]
+            s = dot_nt(q, k) * scale + bias[n]
+            s = jnp.where(live, s, -1000000000.0)
+            e = jnp.exp(s - jnp.max(s, axis=-1, keepdims=True))
+            p = e * (1.0 / jnp.sum(e, axis=-1, keepdims=True))
+            probs[b * heads + n] = p
+            attended[rows, n * dh : (n + 1) * dh] = dot_nn(p.astype(BF16), v).astype(BF16)
+
+
+def attend_back_kernel(
+    heads, dh, per, faces, arrival, packed, window, hid, probs, mixed, wq,
+    own, ret, gw, gp, acc,
+):
+    bricks = packed.shape[0] // per
+    scale = 1.0 / math.sqrt(dh)
+
+    def clear(s, c):
+        ret[s] = jnp.zeros(ret.shape[1:], BF16)
+        return c
+
+    lax.fori_loop(0, ret.shape[0], clear, 0)
+    gp[...] = jnp.zeros(gp.shape, BF16)
+    for b in range(bricks):
+        rows = slice(b * per, (b + 1) * per)
+        for n in range(heads):
+            q = packed[rows, n * 3 * dh : n * 3 * dh + dh]
+            k = window[b, :, n * 2 * dh : n * 2 * dh + dh]
+            v = window[b, :, n * 2 * dh + dh : (n + 1) * 2 * dh]
+            p = probs[b * heads + n]
+            g = mixed[rows, n * dh : (n + 1) * dh]
+            dp = dot_nt(g, v)
+            low = (p * (dp - jnp.sum(p * dp, axis=-1, keepdims=True))).astype(BF16)
+            at = n * 3 * dh
+            gp[0:per, at : at + dh] = (dot_nn(low, k) * scale).astype(BF16)
+            gp[:, at + dh : at + 2 * dh] = (dot_tn(low, q) * scale).astype(BF16)
+            gp[:, at + 2 * dh : at + 3 * dh] = dot_tn(p.astype(BF16), g).astype(BF16)
+        back = dot_nt(gp[...], wq[...])
+        own[rows, :] = back[0:per]
+        for j in range(faces):
+            ret[arrival[b * faces + j]] = back[(j + 1) * per : (j + 2) * per].astype(BF16)
+        term = dot_tn(hid[b], gp[...])
+        acc[...] = term if b == 0 else acc[...] + term
+    gw[...] = acc[...].astype(BF16)
+
+
+def return_kernel(
+    count, send, tok, gain, gout, own, ret, gw, up_pre, wup_hbm, wdn_hbm,
+    out, gw_out,
+    sib, msg, inbox, part, pmsg, pbox, result, g1a, g1b, s1a, s1b, g2a, g2b, s2, g3, wup, wdn,
+    wsem, bs, br, ssem, rsem, xs, xr,
+):
+    me, core = lax.axis_index("tok"), lax.axis_index("mdl")
+    other = 1 - core
+    bricks, per, width = tok.shape
+    slots = ret.shape[1]
+    half = per // 2
+    mine = pl.ds(pl.multiple_of(core * half, half), half)
+    theirs = pl.ds(pl.multiple_of(other * half, half), half)
+    x, y, z = lax.rem(me, 2), lax.rem(me // 2, 2), me // 4
+    xn, yn = me + 1 - 2 * x, me + 2 - 4 * y
+    loads = [
+        pltpu.make_async_copy(a, b, wsem.at[i])
+        for i, (a, b) in enumerate(((wup_hbm, wup), (wdn_hbm, wdn)))
+    ]
+    for load in loads:
+        load.start()
+    greet(me, count, other)
+    cut = gw.shape[-1] // 2
+
+    def sib_copy(i):
+        peer = lax.rem(me + i, count)
+        return remote(ret.at[peer, :, theirs, :], sib.at[i], bs.at[i], br.at[i], {"mdl": other})
+
+    def give(i, c):
+        sib_copy(i).start()
+        return c
+
+    lax.fori_loop(0, count, give, 0)
+    one_a = remote(gw.at[:, :, 1 - x, :, pl.ds(0, cut)], g1a, xs.at[0], xr.at[0], {"tok": xn})
+    one_b = remote(gw.at[:, 1 - y, :, :, pl.ds(cut, cut)], g1b, xs.at[1], xr.at[1], {"tok": yn})
+
+    def out_copy(i):
+        peer = lax.rem(me + i, count)
+        return remote(msg.at[i], inbox.at[i], ssem.at[i], rsem.at[i], {"tok": peer})
+
+    def launch(i, c):
+        peer = lax.rem(me + i, count)
+        sib_copy(i).wait()
+        msg[i] = (ret[peer, :, mine, :].astype(F32) + sib[i].astype(F32)).astype(BF16)
+        out_copy(i).start()
+        return c
+
+    one_a.start()
+    one_b.start()
+    lax.fori_loop(1, count, launch, 0)
+    sib_copy(0).wait()
+    inbox[0] = (ret[me, :, mine, :].astype(F32) + sib[0].astype(F32)).astype(BF16)
+
+    for load in loads:
+        load.wait()
+    ff = wup.shape[1]
+    step = ff // 3
+
+    def feed(n):
+        cols = slice(n * step, (n + 1) * step)
+        act = dot_nt(gout[...], wdn[cols, :])
+        pre = (gelu_slope(up_pre[:, cols]) * act).astype(BF16)
+        term = dot_nt(pre, wup[:, cols])
+        part[...] = part[...] + term
+
+    part[...] = own[...]
+    feed(0)
+    feed(1)
+    one_a.wait()
+    one_b.wait()
+    s1a[...] = (gw[:, :, x, :, 0:cut].astype(F32) + g1a[...].astype(F32)).astype(BF16)
+    s1b[...] = (gw[:, y, :, :, cut : 2 * cut].astype(F32) + g1b[...].astype(F32)).astype(BF16)
+    two_a = remote(s1a.at[:, 1 - y], g2a, xs.at[2], xr.at[2], {"tok": yn})
+    two_b = remote(s1b.at[:, 1 - x], g2b, xs.at[3], xr.at[3], {"tok": xn})
+    two_a.start()
+    two_b.start()
+    feed(2)
+    for b in range(bricks):
+        pmsg[b] = part[pl.ds(pl.multiple_of(b * per + other * half, half), half), :].astype(BF16)
+    swap_part = remote(pmsg, pbox, xs.at[4], xr.at[4], {"mdl": other})
+    swap_part.start()
+    two_a.wait()
+    two_b.wait()
+    s2[:, :, 0:cut] = (s1a[:, y].astype(F32) + g2a[...].astype(F32)).astype(BF16)
+    s2[:, :, cut : 2 * cut] = (s1b[:, x].astype(F32) + g2b[...].astype(F32)).astype(BF16)
+    last = []
+    for d in range(1, 4):
+        copy = remote(
+            s2.at[lax.rem(z + d, 4)], g3.at[d - 1], xs.at[5 + d], xr.at[5 + d],
+            {"tok": lax.rem(me + 4 * d, count)},
+        )
+        copy.start()
+        last.append(copy)
+    swap_part.wait()
+    for b in range(bricks):
+        result[b] = part[pl.ds(pl.multiple_of(b * per + core * half, half), half), :] + pbox[b].astype(F32)
+
+    def take(i, c):
+        source = lax.rem(me - i + count, count)
+
+        @pl.when(i > 0)
+        def _():
+            remote(msg.at[i], inbox.at[i], ssem.at[i], rsem.at[i], {"tok": source}).wait()
+
+        for k in range(slots):
+            value = inbox[i, k].astype(F32)
+            brick = send[source * slots + k]
+            for b in range(bricks):
+                result[b] = result[b] + jnp.where(brick == b, 1.0, 0.0) * value
+        return c
+
+    lax.fori_loop(0, count, take, 0)
+    for b in range(bricks):
+        v = tok[b, mine, :].astype(F32)
+        inv = lax.rsqrt(jnp.mean(v * v, axis=-1, keepdims=True) + norm_eps)
+        normed = v * inv
+        g = result[b] * gain[...]
+        base = gout[pl.ds(pl.multiple_of(b * per + core * half, half), half), :].astype(F32)
+        out[b, mine, :] = (
+            base + inv * (g - normed * jnp.mean(g * normed, axis=-1, keepdims=True))
+        ).astype(BF16)
+    share = remote(out.at[:, mine, :], out.at[:, mine, :], xs.at[5], xr.at[5], {"mdl": other})
+    share.start()
+    for copy in last:
+        copy.wait()
+    gw_out[...] = (
+        s2[z].astype(F32) + g3[0].astype(F32) + g3[1].astype(F32) + g3[2].astype(F32)
+    )
+    share.wait_send()
+    remote(out.at[:, theirs, :], out.at[:, theirs, :], xs.at[5], xr.at[5], {"mdl": other}).wait_recv()
+
+
+def body(
+    tokens,
+    cotangent,
+    norm_gain,
+    w_qkv,
+    w_out,
+    w_up,
+    w_down,
+    w_disp,
+    rel_bias,
+    face_source,
+    face_live,
+    send_bricks,
+):
+    bricks, per, width = tokens.shape
+    rows = bricks * per
+    heads = rel_bias.shape[0]
+    dh = w_out.shape[0] // heads
+    faces = face_source.shape[1]
+    devices = lax.axis_size("tok")
+    slots = send_bricks.shape[2]
+    total = devices * slots
+    kv = heads * 2 * dh
+    wide = heads * 3 * dh
+    span = (faces + 1) * per
+    ff = w_up.shape[1]
+    half = per // 2
+    send = send_bricks.reshape(-1)
+    sources = face_source.reshape(-1)
+    matches = (sources[:, None] == sources[None, :]).astype(jnp.int32)
+    count = sources.shape[0]
+    before = jnp.arange(count)[None, :] < jnp.arange(count)[:, None]
+    arrival = sources * slots + jnp.sum(jnp.where(before, matches, 0), axis=1)
+    seen = jnp.concatenate([jnp.ones((bricks, 1), jnp.int32), face_live], axis=1)
+    seen = jnp.repeat(seen, per, axis=1)
+    gain = norm_gain.reshape(1, width)
+    flat = tokens.reshape(rows, width)
+    any_spec = pl.BlockSpec(memory_space=pl.ANY)
+    dma = pltpu.SemaphoreType.DMA
+
+    def shape(dims, kind=BF16):
+        return jax.ShapeDtypeStruct(dims, kind)
+
+    def talk(ident):
+        return pltpu.CompilerParams(
+            vmem_limit_bytes=48 << 20, collective_id=ident, has_side_effects=True
+        )
+
+    recv, hidden, packed, up_pre, part_ffn = pl.pallas_call(
+        functools.partial(gather_kernel, devices),
+        out_shape=(
+            shape((devices, slots, per, width)),
+            shape((rows, width)),
+            shape((rows, wide)),
+            shape((rows, ff), F32),
+            shape((rows, width), F32),
+        ),
+        in_specs=[SM, VM, VM, any_spec, any_spec, any_spec],
+        out_specs=(VM,) * 5,
+        scratch_shapes=[
+            pltpu.VMEM((devices - 1, slots, half, width), BF16),
+            pltpu.VMEM((width, wide), BF16),
+            pltpu.VMEM((width, ff), BF16),
+            pltpu.VMEM((ff, width), BF16),
+            dma((3,)),
+            dma((devices - 1,)),
+            dma((devices - 1,)),
+            dma((devices - 1,)),
+            dma((devices - 1,)),
+        ],
+        compiler_params=talk(2),
+        name="gather",
+    )(send, tokens, gain, w_qkv, w_up, w_down)
+
+    attended, probs, window, hid = pl.pallas_call(
+        functools.partial(attend_kernel, heads, dh, per, faces),
+        out_shape=(
+            shape((rows, heads * dh)),
+            shape((bricks * heads, per, span), F32),
+            shape((bricks, span, kv)),
+            shape((bricks, span, width)),
+        ),
+        in_specs=[SM] + [VM] * 7,
+        out_specs=(VM,) * 4,
+        scratch_shapes=[pltpu.VMEM((faces * per, width), BF16)],
+        compiler_params=PARAMS,
+        name="attend",
+    )(arrival, hidden, packed, recv.reshape(total, per, width), gain, w_qkv, rel_bias, seen)
+
+    part_out = part_ffn + jnp.dot(attended, w_out, preferred_element_type=F32)
+    folding, grad_out = pl.pallas_call(
+        fold_swap_kernel,
+        out_shape=(shape((1, rows), F32), shape((rows, width))),
+        in_specs=[VM] * 4,
+        out_specs=(VM, VM),
+        scratch_shapes=[pltpu.VMEM((rows, width), F32), dma, dma],
+        compiler_params=talk(0),
+        name="fold_swap",
+    )(flat, part_out, cotangent.reshape(rows, width), w_disp)
+    grad_mixed = jnp.dot(grad_out, w_out.T, preferred_element_type=F32).astype(BF16)
+
+    own, ret, gw = pl.pallas_call(
+        functools.partial(attend_back_kernel, heads, dh, per, faces),
+        out_shape=(
+            shape((rows, width), F32),
+            shape((total, per, width)),
+            shape((width, wide)),
+        ),
+        in_specs=[SM] + [VM] * 6,
+        out_specs=(VM,) * 3,
+        scratch_shapes=[pltpu.VMEM((span, wide), BF16), pltpu.VMEM((width, wide), F32)],
+        compiler_params=PARAMS,
+        name="attend_back",
+    )(arrival, packed, window, hid, probs, grad_mixed, w_qkv)
+
+    piece = width // devices
+    cut = wide // 2
+    grad_tokens, grad_weight = pl.pallas_call(
+        functools.partial(return_kernel, devices),
+        out_shape=(shape((bricks, per, width)), shape((piece, wide), F32)),
+        in_specs=[SM] + [VM] * 7 + [any_spec] * 2,
+        out_specs=(VM, VM),
+        scratch_shapes=[
+            pltpu.VMEM((devices, slots, half, width), BF16),
+            pltpu.VMEM((devices, slots, half, width), BF16),
+            pltpu.VMEM((devices, slots, half, width), BF16),
+            pltpu.VMEM((rows, width), F32),
+            pltpu.VMEM((bricks, half, width), BF16),
+            pltpu.VMEM((bricks, half, width), BF16),
+            pltpu.VMEM((bricks, half, width), F32),
+            pltpu.VMEM((4, 2, piece, cut), BF16),
+            pltpu.VMEM((4, 2, piece, cut), BF16),
+            pltpu.VMEM((4, 2, piece, cut), BF16),
+            pltpu.VMEM((4, 2, piece, cut), BF16),
+            pltpu.VMEM((4, piece, cut), BF16),
+            pltpu.VMEM((4, piece, cut), BF16),
+            pltpu.VMEM((4, piece, wide), BF16),
+            pltpu.VMEM((3, piece, wide), BF16),
+            pltpu.VMEM((width, ff), BF16),
+            pltpu.VMEM((ff, width), BF16),
+            dma((2,)),
+            dma((devices,)),
+            dma((devices,)),
+            dma((devices,)),
+            dma((devices,)),
+            dma((9,)),
+            dma((9,)),
+        ],
+        compiler_params=talk(1),
+        name="give_back",
+    )(
+        send,
+        tokens,
+        gain,
+        grad_out,
+        own,
+        ret.reshape(devices, slots, per, width),
+        gw.reshape(4, 2, 2, piece, wide),
+        up_pre,
+        w_up,
+        w_down,
+    )
+    return (folding.reshape(bricks, per), grad_tokens, grad_weight)
+
+
 def solution(mesh):
     return jax.shard_map(
-        body,
+        body if mesh.shape["tok"] == 16 and mesh.shape["mdl"] == 2 else body_wide,
         mesh=mesh,
         in_specs=(
             P("tok", None, None),

time: 180 us -> 149 us (0.83)
  Pallas kernels: 25.6 us -> 123 us
  blocking collectives: 58.9 us -> 0 us
  waiting for transfers between devices: 50 us -> 0 us
  starting transfers between devices: 12.9 us -> 0 us
  matrix products: 11.8 us -> 0.56 us
  local copies, waits for them, and re-layouts: 14.1 us -> 23.1 us
  other arithmetic: 4.85 us -> 0.85 us
    pallas_call x6 -> x5, Pallas kernels: 25.6 us -> 123 us  [the longest x1 63.1 us: body(): pl.pallas_call(functools.partial(return_kernel, devices), out_shape=(shap...]
    all_to_all x1 -> x0, blocking collectives: 58.9 us -> none  [body(): lax.all_to_all(returning, 'tok', split_axis=0, concat_axis=0, tiled=True)]
    all_to_all x2 -> x0, waiting for transfers between devices: 50 us -> none  [the longest x1 35.1 us: body(): lax.all_to_all(outgoing, 'tok', split_axis=0, concat_axis=0, tiled=True)]
    all_to_all x2 -> x0, starting transfers between devices: 12.9 us -> none  [the longest x1 8.49 us: body(): lax.all_to_all(outgoing, 'tok', split_axis=0, concat_axis=0, tiled=True)]
    dot_general x5 -> x0, matrix products: 11.2 us -> none  [the longest x1 5.17 us: body(): part_up = jnp.dot(grad_pre, w_up.T, preferred_element_type=F32)]
    unnamed x43 -> x46, local copies, waits for them, and re-layouts: 11.1 us -> 20.7 us
    reduce_sum x1 -> x0, other arithmetic: 2.1 us -> none  [body(): grad_weight = jnp.sum(terms.astype(F32), axis=0)]
  transfers between devices with their start and end apart: 2 -> 0, of which waited for: 2 -> 0; matrix products, arithmetic and copies ran while one was open for 9% -> 0% of each run, Pallas kernels for 1% -> 0%
where the time goes in v2:
time: 149 us
  Pallas kernels  123 us (83%)
  local copies, waits for them, and re-layouts  23.1 us (16%)
    pallas_call x1, Pallas kernels, body(): pl.pallas_call(functools.partial(return_kernel, devices), out_shape=(shap...  63.1 us
    pallas_call x1, Pallas kernels, body(): pl.pallas_call(functools.partial(gather_kernel, devices), out_shape=(shap...  35.3 us
    unnamed x46, local copies, waits for them, and re-layouts  20.7 us
    pallas_call x1, Pallas kernels, body(): pl.pallas_call(functools.partial(attend_back_kernel, heads, dh, per, face...  12.5 us
    pallas_call x1, Pallas kernels, body(): pl.pallas_call(functools.partial(attend_kernel, heads, dh, per, faces), o...  9.26 us
    pallas_call x1, Pallas kernels, body(): pl.pallas_call(fold_swap_kernel, out_shape=(shape((1, rows), F32), shape(...  3.28 us

profile of v2, /device:TPU:0, one launch (start us, length us, event | category | flops | bytes accessed | tf_op | source)
XLA Modules:
  0.0 148.7 jit_solution(13228144491003649371)
XLA Ops:
  0.6 0.7 reshape.40.gain
  1.4 0.8 copy.19
  2.2 1.3 copy-done.1
  3.5 1.0 copy-done.3
  4.5 35.3 %gather.1 = (bf16[16,2,64,768]{3,2,1,0:T(8,128)(2,1)}, bf16[256,768]{1,0:T(8,128)(2,1)S(1)}, bf16[256,768]{1,0:T(8,128)(2,1)S(1)}, f32[256,1536]{1,0:T(8,128)S(1)}, f32[256,768]{1,0:T(8,128)S(1)}) custom-call(s32[32]{0:T(128)S(1)} %reshape.39.send, bf16[4,64,768]{2,1,0:T(8,128)(2,1)S(1)} %copy-done.3, f32[1,768]{1,0:T(1,128)S(1)} %reshape.40.gain, ...), custom_call_target="tpu_custom_call" | custom-call | tf_op jit(solution)/shard_map/gather/pallas_call | solution.py:739
  39.8 1.2 copy-done.13
  41.0 0.9 copy-done.15
  42.4 1.9 %copy-done.5 = bf16[16,2,64,768]{3,2,1,0:T(8,128)(2,1)S(1)} copy-done((bf16[16,2,64,768]{3,2,1,0:T(8,128)(2,1)S(1)}, bf16[16,2,64,768]{3,2,1,0:T(8,128)(2,1)}, u32[]{:S(2)}) %copy-start.5) | copy-done | bytes 3145752
  44.3 1.0 copy-done.17
  45.4 9.3 %attend.1 = (bf16[256,256]{1,0:T(8,128)(2,1)S(1)}, f32[16,64,448]{2,1,0:T(8,128)S(1)}, bf16[4,448,512]{2,1,0:T(8,128)(2,1)S(1)}, bf16[4,448,768]{2,1,0:T(8,128)(2,1)S(1)}) custom-call(s32[24]{0:T(128)S(1)} %multiply_add_fusion.arrival, bf16[256,768]{1,0:T(8,128)(2,1)S(1)} %get-tuple-element.20.hidden, bf16[256,768]{1,0:T(8,128)(2,1)S(1)} %get-tuple-element.21.packed, ...), custom_call_target="tpu_custom_call" | custom-call | tf_op jit(solution)/shard_map/attend/pallas_call | solution.py:765
  54.6 1.6 %copy-done.7 = bf16[4,448,768]{2,1,0:T(8,128)(2,1)} copy-done((bf16[4,448,768]{2,1,0:T(8,128)(2,1)}, bf16[4,448,768]{2,1,0:T(8,128)(2,1)S(1)}, u32[]{:S(2)}) %copy-start.7) | copy-done | bytes 2752536
  56.2 1.4 copy-done.9
  57.6 1.3 copy-done.11
  59.2 1.1 copy.20.w_disp
  60.3 1.1 copy-done.18
  61.5 3.3 %fold_swap.1 = (f32[1,256]{1,0:T(1,128)S(1)}, bf16[256,768]{1,0:T(8,128)(2,1)S(1)}) custom-call(bf16[256,768]{1,0:T(8,128)(2,1)S(1)} %bitcast.9, f32[256,768]{1,0:T(8,128)S(1)} %convolution_add_fusion.part, bf16[256,768]{1,0:T(8,128)(2,1)S(1)} %bitcast.13, bf16[768,192]{1,0:T(8,128)(2,1)S(1)} %copy.20.w_disp), custom_call_target="tpu_custom_call" | custom-call | tf_op jit(solution)/shard_map/fold_swap/pallas_call | solution.py:781
  65.1 1.6 %copy-done.10 = f32[16,64,448]{2,1,0:T(8,128)S(1)} copy-done((f32[16,64,448]{2,1,0:T(8,128)S(1)}, f32[16,64,448]{2,1,0:T(8,128)}, u32[]{:S(2)}) %copy-start.10) | copy-done | bytes 1835032
  66.7 1.5 %copy-done.12 = bf16[4,448,512]{2,1,0:T(8,128)(2,1)S(1)} copy-done((bf16[4,448,512]{2,1,0:T(8,128)(2,1)S(1)}, bf16[4,448,512]{2,1,0:T(8,128)(2,1)}, u32[]{:S(2)}) %copy-start.12) | copy-done | bytes 1835032
  68.2 12.5 %attend_back.1 = (f32[256,768]{1,0:T(8,128)S(1)}, bf16[32,64,768]{2,1,0:T(8,128)(2,1)S(1)}, bf16[768,768]{1,0:T(8,128)(2,1)S(1)}) custom-call(s32[24]{0:T(128)S(1)} %multiply_add_fusion.arrival, bf16[256,768]{1,0:T(8,128)(2,1)S(1)} %get-tuple-element.21.packed, bf16[4,448,512]{2,1,0:T(8,128)(2,1)S(1)} %copy-done.12, bf16[4,448,768]{2,1,0:T(8,128)(2,1)S(1)} %copy-done.8, ...), custom_call_target="tpu_custom_call" | custom-call | tf_op jit(solution)/shard_map/attend_back/pallas_call | solution.py:792
  80.7 1.6 %copy-done.6 = bf16[32,64,768]{2,1,0:T(8,128)(2,1)} copy-done((bf16[32,64,768]{2,1,0:T(8,128)(2,1)}, bf16[32,64,768]{2,1,0:T(8,128)(2,1)S(1)}, u32[]{:S(2)}) %copy-start.6) | copy-done | bytes 3145752
  82.3 63.1 %give_back.1 = (bf16[4,64,768]{2,1,0:T(8,128)(2,1)S(1)}, f32[48,768]{1,0:T(8,128)S(1)}) custom-call(s32[32]{0:T(128)S(1)} %reshape.39.send, bf16[4,64,768]{2,1,0:T(8,128)(2,1)S(1)} %copy-done.4, f32[1,768]{1,0:T(1,128)S(1)} %reshape.40.gain, bf16[256,768]{1,0:T(8,128)(2,1)S(1)} %get-tuple-element.25.gout, f32[256,768]{1,0:T(8,128)S(1)} %get-tuple-element.29.own, ...), custom_call_target="tpu_custom_call" | custom-call | tf_op jit(solution)/shard_map/give_back/pallas_call | solution.py:808
  146.0 0.7 reduce.3
  146.7 0.7 reshape.45
  147.3 0.7 copy.23
  (40 shorter events, 2.4 us)
Async XLA Ops:
  0.6 58.2 %copy-start = (bf16[256,768]{1,0:T(8,128)(2,1)S(1)}, bf16[256,768]{1,0:T(8,128)(2,1)}, u32[]{:S(2)}) copy-start(bf16[256,768]{1,0:T(8,128)(2,1)} %param.16) | copy-start | bytes 1179652
  2.2 1.3 copy-start.1
  3.5 1.0 copy-start.3
  4.5 37.4 %copy-start.19 = (s32[4,6]{1,0:T(4,128)S(1)}, s32[4,6]{1,0:T(4,128)}, u32[]{:S(2)}) copy-start(s32[4,6]{1,0:T(4,128)} %param.21) | copy-start | bytes 292
  4.5 37.7 %copy-start.20 = (s32[4,6]{1,0:T(4,128)S(1)}, s32[4,6]{1,0:T(4,128)}, u32[]{:S(2)}) copy-start(s32[4,6]{1,0:T(4,128)} %param.22) | copy-start | bytes 292
  4.5 37.9 %copy-start.2 = (bf16[768,768]{1,0:T(8,128)(2,1)S(1)}, bf16[768,768]{1,0:T(8,128)(2,1)}, u32[]{:S(2)}) copy-start(bf16[768,768]{1,0:T(8,128)(2,1)} %wq.3) | copy-start | bytes 3538948
  39.8 1.2 copy-start.13
  41.0 0.9 copy-start.15
  42.4 1.9 %copy-start.5 = (bf16[16,2,64,768]{3,2,1,0:T(8,128)(2,1)S(1)}, bf16[16,2,64,768]{3,2,1,0:T(8,128)(2,1)}, u32[]{:S(2)}) copy-start(bf16[16,2,64,768]{3,2,1,0:T(8,128)(2,1)} %get-tuple-element.22) | copy-start | bytes 9437188
  44.3 1.0 copy-start.17
  45.4 13.5 %copy-start.16 = (f32[256,768]{1,0:T(8,128)S(1)}, f32[256,768]{1,0:T(8,128)}, u32[]{:S(2)}) copy-start(f32[256,768]{1,0:T(8,128)} %copy-done.15) | copy-start | bytes 2359300
  54.6 1.6 %copy-start.7 = (bf16[4,448,768]{2,1,0:T(8,128)(2,1)}, bf16[4,448,768]{2,1,0:T(8,128)(2,1)S(1)}, u32[]{:S(2)}) copy-start(bf16[4,448,768]{2,1,0:T(8,128)(2,1)S(1)} %get-tuple-element.27.hid) | copy-start | bytes 8257540
  56.2 1.4 copy-start.9
  57.6 1.3 copy-start.11
  58.9 1.4 copy-start.4
  60.3 4.8 %copy-start.8 = (bf16[4,448,768]{2,1,0:T(8,128)(2,1)S(1)}, bf16[4,448,768]{2,1,0:T(8,128)(2,1)}, u32[]{:S(2)}) copy-start(bf16[4,448,768]{2,1,0:T(8,128)(2,1)} %copy-done.7) | copy-start | bytes 8257540
  60.3 1.1 copy-start.18
  65.1 1.6 %copy-start.10 = (f32[16,64,448]{2,1,0:T(8,128)S(1)}, f32[16,64,448]{2,1,0:T(8,128)}, u32[]{:S(2)}) copy-start(f32[16,64,448]{2,1,0:T(8,128)} %copy-done.9) | copy-start | bytes 5505028
  66.7 1.5 %copy-start.12 = (bf16[4,448,512]{2,1,0:T(8,128)(2,1)S(1)}, bf16[4,448,512]{2,1,0:T(8,128)(2,1)}, u32[]{:S(2)}) copy-start(bf16[4,448,512]{2,1,0:T(8,128)(2,1)} %copy-done.11) | copy-start | bytes 5505028
  68.2 14.2 %copy-start.14 = (f32[256,1536]{1,0:T(8,128)S(1)}, f32[256,1536]{1,0:T(8,128)}, u32[]{:S(2)}) copy-start(f32[256,1536]{1,0:T(8,128)} %copy-done.13) | copy-start | bytes 4718596
  80.7 1.7 %copy-start.6 = (bf16[32,64,768]{2,1,0:T(8,128)(2,1)}, bf16[32,64,768]{2,1,0:T(8,128)(2,1)S(1)}, u32[]{:S(2)}) copy-start(bf16[32,64,768]{2,1,0:T(8,128)(2,1)S(1)} %get-tuple-element.30) | copy-start | bytes 9437188

commit v3 on v2

--- a/solution.py
+++ b/solution.py
@@ -416,9 +416,9 @@
 
 
 def gather_kernel(
-    count, send, tok, gain, wq_hbm, wup_hbm, wdn_hbm,
-    recv, hidden, packed, up_pre, part,
-    msg, wq, wup, wdn, wsem, ssem, rsem, fssem, frsem,
+    count, send, tok, gain, row, wq_hbm, wup_hbm, wdn_hbm,
+    recv, hidden, packed, up_pre, part, table,
+    msg, wq, wup, wdn, wsem, ssem, rsem, fssem, frsem, tssem, trsem,
 ):
     me, core = lax.axis_index("tok"), lax.axis_index("mdl")
     other = 1 - core
@@ -446,6 +446,16 @@
         out_copy(i).start()
         return c
 
+    def row_copy(i):
+        peer = lax.rem(me + i + 1, count)
+        return remote(row, table.at[me], tssem.at[i], trsem.at[i], {"tok": peer})
+
+    def tell(i, c):
+        row_copy(i).start()
+        return c
+
+    lax.fori_loop(0, count - 1, tell, 0)
+    table[me] = row[...]
     lax.fori_loop(0, count - 1, launch, 0)
     for k in range(slots):
         recv[me, k] = tok[send[me * slots + k]]
@@ -480,6 +490,9 @@
 
     def finish(i, c):
         out_copy(i).wait_send()
+        row_copy(i).wait_send()
+        source = lax.rem(me - (i + 1) + count, count)
+        remote(row, table.at[source], tssem.at[i], trsem.at[i], {"tok": source}).wait_recv()
         relay_copy(i, mine).wait_send()
         relay_copy(i, theirs).wait_recv()
         return c
@@ -560,7 +573,7 @@
     count, send, tok, gain, gout, own, ret, gw, up_pre, wup_hbm, wdn_hbm,
     out, gw_out,
     sib, msg, inbox, part, pmsg, pbox, result, g1a, g1b, s1a, s1b, g2a, g2b, s2, g3, wup, wdn,
-    wsem, bs, br, ssem, rsem, xs, xr,
+    zmsg, zbox, wsem, bs, br, ssem, rsem, xs, xr, zs, zr,
 ):
     me, core = lax.axis_index("tok"), lax.axis_index("mdl")
     other = 1 - core
@@ -580,34 +593,46 @@
     greet(me, count, other)
     cut = gw.shape[-1] // 2
 
-    def sib_copy(i):
-        peer = lax.rem(me + i, count)
-        return remote(ret.at[peer, :, theirs, :], sib.at[i], bs.at[i], br.at[i], {"mdl": other})
-
-    def give(i, c):
-        sib_copy(i).start()
-        return c
-
-    lax.fori_loop(0, count, give, 0)
+    def plane(q):
+        qx, qy = q & 1, q >> 1
+        return (1 - y if qy else y) * 2 + (1 - x if qx else x)
+
+    def holder(q, j):
+        return lax.rem(z + j, 4) * 4 + plane(q)
+
+    order = (1, 2, 3, 0)
+
+    def sib_copy(q, j):
+        i = q * 4 + j
+        return remote(ret.at[holder(q, j), :, theirs, :], sib.at[i], bs.at[i], br.at[i], {"mdl": other})
+
+    def give(n, c):
+        j = lax.rem(n + 1, 4)
+        for q in order:
+            sib_copy(q, j).start()
+        return c
+
+    lax.fori_loop(0, 4, give, 0)
     one_a = remote(gw.at[:, :, 1 - x, :, pl.ds(0, cut)], g1a, xs.at[0], xr.at[0], {"tok": xn})
     one_b = remote(gw.at[:, 1 - y, :, :, pl.ds(cut, cut)], g1b, xs.at[1], xr.at[1], {"tok": yn})
 
-    def out_copy(i):
-        peer = lax.rem(me + i, count)
-        return remote(msg.at[i], inbox.at[i], ssem.at[i], rsem.at[i], {"tok": peer})
-
-    def launch(i, c):
-        peer = lax.rem(me + i, count)
-        sib_copy(i).wait()
-        msg[i] = (ret[peer, :, mine, :].astype(F32) + sib[i].astype(F32)).astype(BF16)
-        out_copy(i).start()
+    def plane_copy(q, j):
+        i = q * 4 + j
+        return remote(msg.at[i], inbox.at[i], ssem.at[i], rsem.at[i], {"tok": z * 4 + plane(q)})
+
+    def launch(n, c):
+        j = lax.rem(n + 1, 4)
+        for q in order:
+            i = q * 4 + j
+            sib_copy(q, j).wait()
+            msg[i] = (ret[holder(q, j), :, mine, :].astype(F32) + sib[i].astype(F32)).astype(BF16)
+            if q:
+                plane_copy(q, j).start()
         return c
 
     one_a.start()
     one_b.start()
-    lax.fori_loop(1, count, launch, 0)
-    sib_copy(0).wait()
-    inbox[0] = (ret[me, :, mine, :].astype(F32) + sib[0].astype(F32)).astype(BF16)
+    lax.fori_loop(0, 4, launch, 0)
 
     for load in loads:
         load.wait()
@@ -621,9 +646,32 @@
         term = dot_nt(pre, wup[:, cols])
         part[...] = part[...] + term
 
+    def merge(j, brick):
+        total = jnp.zeros((half, width), F32)
+        for q in range(4):
+            for k in range(slots):
+                i = q * 4 + j
+                value = (inbox if q else msg)[i, k].astype(F32)
+                named = send[(holder(0, j) * count + z * 4 + plane(q)) * slots + k]
+                total = total + jnp.where(named == brick, 1.0, 0.0) * value
+        return total
+
+    def z_copy(j):
+        return remote(zmsg.at[j - 1], zbox.at[j - 1], zs.at[j - 1], zr.at[j - 1], {"tok": holder(0, j)})
+
+    def pass_on(j):
+        for q in (1, 2, 3):
+            plane_copy(q, j).wait()
+
+        def one(brick, c):
+            zmsg[j - 1, brick] = merge(j, brick).astype(BF16)
+            return c
+
+        lax.fori_loop(0, bricks, one, 0)
+        z_copy(j).start()
+
     part[...] = own[...]
     feed(0)
-    feed(1)
     one_a.wait()
     one_b.wait()
     s1a[...] = (gw[:, :, x, :, 0:cut].astype(F32) + g1a[...].astype(F32)).astype(BF16)
@@ -632,11 +680,15 @@
     two_b = remote(s1b.at[:, 1 - x], g2b, xs.at[3], xr.at[3], {"tok": xn})
     two_a.start()
     two_b.start()
+    pass_on(1)
+    feed(1)
+    pass_on(2)
     feed(2)
     for b in range(bricks):
         pmsg[b] = part[pl.ds(pl.multiple_of(b * per + other * half, half), half), :].astype(BF16)
     swap_part = remote(pmsg, pbox, xs.at[4], xr.at[4], {"mdl": other})
     swap_part.start()
+    pass_on(3)
     two_a.wait()
     two_b.wait()
     s2[:, :, 0:cut] = (s1a[:, y].astype(F32) + g2a[...].astype(F32)).astype(BF16)
@@ -650,24 +702,18 @@
         copy.start()
         last.append(copy)
     swap_part.wait()
-    for b in range(bricks):
-        result[b] = part[pl.ds(pl.multiple_of(b * per + core * half, half), half), :] + pbox[b].astype(F32)
-
-    def take(i, c):
-        source = lax.rem(me - i + count, count)
-
-        @pl.when(i > 0)
-        def _():
-            remote(msg.at[i], inbox.at[i], ssem.at[i], rsem.at[i], {"tok": source}).wait()
-
-        for k in range(slots):
-            value = inbox[i, k].astype(F32)
-            brick = send[source * slots + k]
-            for b in range(bricks):
-                result[b] = result[b] + jnp.where(brick == b, 1.0, 0.0) * value
-        return c
-
-    lax.fori_loop(0, count, take, 0)
+    for q in (1, 2, 3):
+        plane_copy(q, 0).wait()
+
+    def settle(b, c):
+        at = pl.ds(pl.multiple_of(b * per + core * half, half), half)
+        result[b] = part[at, :] + pbox[b].astype(F32) + merge(0, b)
+        return c
+
+    lax.fori_loop(0, bricks, settle, 0)
+    for j in range(1, 4):
+        z_copy(j).wait()
+    result[...] = result[...] + zbox[0].astype(F32) + zbox[1].astype(F32) + zbox[2].astype(F32)
     for b in range(bricks):
         v = tok[b, mine, :].astype(F32)
         inv = lax.rsqrt(jnp.mean(v * v, axis=-1, keepdims=True) + norm_eps)
@@ -716,6 +762,7 @@
     ff = w_up.shape[1]
     half = per // 2
     send = send_bricks.reshape(-1)
+    row = jnp.zeros((8, 128), jnp.int32).at[0, : devices * slots].set(send)
     sources = face_source.reshape(-1)
     matches = (sources[:, None] == sources[None, :]).astype(jnp.int32)
     count = sources.shape[0]
@@ -736,7 +783,7 @@
             vmem_limit_bytes=48 << 20, collective_id=ident, has_side_effects=True
         )
 
-    recv, hidden, packed, up_pre, part_ffn = pl.pallas_call(
+    recv, hidden, packed, up_pre, part_ffn, table = pl.pallas_call(
         functools.partial(gather_kernel, devices),
         out_shape=(
             shape((devices, slots, per, width)),
@@ -744,9 +791,10 @@
             shape((rows, wide)),
             shape((rows, ff), F32),
             shape((rows, width), F32),
+            shape((devices, 8, 128), jnp.int32),
         ),
-        in_specs=[SM, VM, VM, any_spec, any_spec, any_spec],
-        out_specs=(VM,) * 5,
+        in_specs=[SM, VM, VM, VM, any_spec, any_spec, any_spec],
+        out_specs=(VM,) * 6,
         scratch_shapes=[
             pltpu.VMEM((devices - 1, slots, half, width), BF16),
             pltpu.VMEM((width, wide), BF16),
@@ -757,10 +805,12 @@
             dma((devices - 1,)),
             dma((devices - 1,)),
             dma((devices - 1,)),
+            dma((devices - 1,)),
+            dma((devices - 1,)),
         ],
         compiler_params=talk(2),
         name="gather",
-    )(send, tokens, gain, w_qkv, w_up, w_down)
+    )(send, tokens, gain, row, w_qkv, w_up, w_down)
 
     attended, probs, window, hid = pl.pallas_call(
         functools.partial(attend_kernel, heads, dh, per, faces),
@@ -828,6 +878,8 @@
             pltpu.VMEM((3, piece, wide), BF16),
             pltpu.VMEM((width, ff), BF16),
             pltpu.VMEM((ff, width), BF16),
+            pltpu.VMEM((3, bricks, half, width), BF16),
+            pltpu.VMEM((3, bricks, half, width), BF16),
             dma((2,)),
             dma((devices,)),
             dma((devices,)),
@@ -835,11 +887,13 @@
             dma((devices,)),
             dma((9,)),
             dma((9,)),
+            dma((3,)),
+            dma((3,)),
         ],
         compiler_params=talk(1),
         name="give_back",
     )(
-        send,
+        table[:, 0, : devices * slots].reshape(-1),
         tokens,
         gain,
         grad_out,

time: 149 us -> 145 us (0.973)
  Pallas kernels: 123 us -> 116 us
  local copies, waits for them, and re-layouts: 23.1 us -> 26 us
    pallas_call x1, Pallas kernels: 63.1 us -> 54.4 us  [body(): pl.pallas_call(functools.partial(return_kernel, devices), out_shape=(shap...]
    unnamed x46 -> x42, local copies, waits for them, and re-layouts: 20.7 us -> 22.1 us
where the time goes in v3:
time: 145 us; the launch traced here: 144 us
  Pallas kernels  116 us (80%)
  local copies, waits for them, and re-layouts  26 us (18%)
    pallas_call x1, Pallas kernels, body(): pl.pallas_call(functools.partial(return_kernel, devices), out_shape=(shap...  54.4 us
    pallas_call x1, Pallas kernels, body(): pl.pallas_call(functools.partial(gather_kernel, devices), out_shape=(shap...  36.5 us
    unnamed x42, local copies, waits for them, and re-layouts  22.1 us
    pallas_call x1, Pallas kernels, body(): pl.pallas_call(functools.partial(attend_back_kernel, heads, dh, per, face...  12.5 us
    pallas_call x1, Pallas kernels, body(): pl.pallas_call(functools.partial(attend_kernel, heads, dh, per, faces), o...  9.19 us
    pallas_call x1, Pallas kernels, body(): pl.pallas_call(fold_swap_kernel, out_shape=(shape((1, rows), F32), shape(...  3.27 us

profile of v3, /device:TPU:0, one launch (start us, length us, event | category | flops | bytes accessed | tf_op | source)
XLA Modules:
  0.0 144.1 jit_solution(13344952436175448906)
XLA Ops:
  0.6 0.8 reshape.74
  1.6 0.8 concatenate.5
  3.1 0.8 copy.21
  4.2 1.1 copy.23.w_disp
  5.3 1.3 copy-done.1
  6.6 1.0 copy-done.3
  7.6 36.5 %gather.1 = (bf16[16,2,64,768]{3,2,1,0:T(8,128)(2,1)}, bf16[256,768]{1,0:T(8,128)(2,1)S(1)}, bf16[256,768]{1,0:T(8,128)(2,1)S(1)}, f32[256,1536]{1,0:T(8,128)S(1...) custom-call(s32[32]{0:T(128)S(1)} %reshape.71.send, bf16[4,64,768]{2,1,0:T(8,128)(2,1)S(1)} %copy-done.3, ...), custom_call_target="tpu_custom_call" | custom-call | tf_op jit(solution)/shard_map/gather/pallas_call | solution.py:786
  44.2 1.2 copy-done.13
  45.3 0.9 copy-done.15
  46.4 1.9 %copy-done.5 = bf16[16,2,64,768]{3,2,1,0:T(8,128)(2,1)S(1)} copy-done((bf16[16,2,64,768]{3,2,1,0:T(8,128)(2,1)S(1)}, bf16[16,2,64,768]{3,2,1,0:T(8,128)(2,1)}, u32[]{:S(2)}) %copy-start.5) | copy-done | bytes 3145752
  48.3 1.0 copy-done.17
  49.3 9.2 %attend.1 = (bf16[256,256]{1,0:T(8,128)(2,1)S(1)}, f32[16,64,448]{2,1,0:T(8,128)S(1)}, bf16[4,448,512]{2,1,0:T(8,128)(2,1)S(1)}, bf16[4,448,768]{2,1,0:T(8,128)(2,1)S(1)}) custom-call(s32[24]{0:T(128)S(1)} %multiply_add_fusion.arrival, bf16[256,768]{1,0:T(8,128)(2,1)S(1)} %get-tuple-element.33.hidden, bf16[256,768]{1,0:T(8,128)(2,1)S(1)} %get-tuple-element.34.packed, ...), custom_call_target="tpu_custom_call" | custom-call | tf_op jit(solution)/shard_map/attend/pallas_call | solution.py:815
  58.5 1.5 %copy-done.7 = bf16[4,448,768]{2,1,0:T(8,128)(2,1)} copy-done((bf16[4,448,768]{2,1,0:T(8,128)(2,1)}, bf16[4,448,768]{2,1,0:T(8,128)(2,1)S(1)}, u32[]{:S(2)}) %copy-start.7) | copy-done | bytes 2752536
  60.0 1.4 copy-done.9
  61.4 1.3 copy-done.11
  63.0 0.7 copy-done.4
  63.8 3.3 %fold_swap.1 = (f32[1,256]{1,0:T(1,128)S(1)}, bf16[256,768]{1,0:T(8,128)(2,1)S(1)}) custom-call(bf16[256,768]{1,0:T(8,128)(2,1)S(1)} %bitcast.9, f32[256,768]{1,0:T(8,128)S(1)} %convolution_add_fusion.part, bf16[256,768]{1,0:T(8,128)(2,1)S(1)} %bitcast.13, bf16[768,192]{1,0:T(8,128)(2,1)S(1)} %copy.23.w_disp), custom_call_target="tpu_custom_call" | custom-call | tf_op jit(solution)/shard_map/fold_swap/pallas_call | solution.py:831
  69.2 1.8 %copy-done.8 = bf16[4,448,768]{2,1,0:T(8,128)(2,1)S(1)} copy-done((bf16[4,448,768]{2,1,0:T(8,128)(2,1)S(1)}, bf16[4,448,768]{2,1,0:T(8,128)(2,1)}, u32[]{:S(2)}) %copy-start.8) | copy-done | bytes 2752536
  71.0 1.6 %copy-done.10 = f32[16,64,448]{2,1,0:T(8,128)S(1)} copy-done((f32[16,64,448]{2,1,0:T(8,128)S(1)}, f32[16,64,448]{2,1,0:T(8,128)}, u32[]{:S(2)}) %copy-start.10) | copy-done | bytes 1835032
  72.6 1.5 %copy-done.12 = bf16[4,448,512]{2,1,0:T(8,128)(2,1)S(1)} copy-done((bf16[4,448,512]{2,1,0:T(8,128)(2,1)S(1)}, bf16[4,448,512]{2,1,0:T(8,128)(2,1)}, u32[]{:S(2)}) %copy-start.12) | copy-done | bytes 1835032
  74.1 12.5 %attend_back.1 = (f32[256,768]{1,0:T(8,128)S(1)}, bf16[32,64,768]{2,1,0:T(8,128)(2,1)S(1)}, bf16[768,768]{1,0:T(8,128)(2,1)S(1)}) custom-call(s32[24]{0:T(128)S(1)} %multiply_add_fusion.arrival, bf16[256,768]{1,0:T(8,128)(2,1)S(1)} %get-tuple-element.34.packed, bf16[4,448,512]{2,1,0:T(8,128)(2,1)S(1)} %copy-done.12, bf16[4,448,768]{2,1,0:T(8,128)(2,1)S(1)} %copy-done.8, ...), custom_call_target="tpu_custom_call" | custom-call | tf_op jit(solution)/shard_map/attend_back/pallas_call | solution.py:842
  86.6 1.6 %copy-done.6 = bf16[32,64,768]{2,1,0:T(8,128)(2,1)} copy-done((bf16[32,64,768]{2,1,0:T(8,128)(2,1)}, bf16[32,64,768]{2,1,0:T(8,128)(2,1)S(1)}, u32[]{:S(2)}) %copy-start.6) | copy-done | bytes 3145752
  88.3 54.4 %give_back.1 = (bf16[4,64,768]{2,1,0:T(8,128)(2,1)S(1)}, f32[48,768]{1,0:T(8,128)S(1)}) custom-call(s32[512]{0:T(512)S(1)} %reshape_squeeze.3.send, bf16[4,64,768]{2,1,0:T(8,128)(2,1)S(1)} %copy-done.4, f32[1,768]{1,0:T(1,128)S(1)} %reshape.72.gain, bf16[256,768]{1,0:T(8,128)(2,1)S(1)} %get-tuple-element.39.gout, f32[256,768]{1,0:T(8,128)S(1)} %get-tuple-element.43.own, ...), custom_call_target="tpu_custom_call" | custom-call | tf_op jit(solution)/shard_map/give_back/pallas_call | solution.py:858
  142.7 0.7 copy.26
  (40 shorter events, 4.5 us)
Async XLA Ops:
  0.6 62.1 %copy-start = (bf16[256,768]{1,0:T(8,128)(2,1)S(1)}, bf16[256,768]{1,0:T(8,128)(2,1)}, u32[]{:S(2)}) copy-start(bf16[256,768]{1,0:T(8,128)(2,1)} %param.18) | copy-start | bytes 1179652
  5.3 1.3 copy-start.1
  6.6 1.0 copy-start.3
  7.6 38.8 %copy-start.2 = (bf16[768,768]{1,0:T(8,128)(2,1)S(1)}, bf16[768,768]{1,0:T(8,128)(2,1)}, u32[]{:S(2)}) copy-start(bf16[768,768]{1,0:T(8,128)(2,1)} %wq.3) | copy-start | bytes 3538948
  44.1 1.2 copy-start.13
  45.3 0.9 copy-start.15
  46.4 1.9 %copy-start.5 = (bf16[16,2,64,768]{3,2,1,0:T(8,128)(2,1)S(1)}, bf16[16,2,64,768]{3,2,1,0:T(8,128)(2,1)}, u32[]{:S(2)}) copy-start(bf16[16,2,64,768]{3,2,1,0:T(8,128)(2,1)} %get-tuple-element.35) | copy-start | bytes 9437188
  48.3 1.0 copy-start.17
  49.3 13.4 %copy-start.16 = (f32[256,768]{1,0:T(8,128)S(1)}, f32[256,768]{1,0:T(8,128)}, u32[]{:S(2)}) copy-start(f32[256,768]{1,0:T(8,128)} %copy-done.15) | copy-start | bytes 2359300
  58.5 1.5 %copy-start.7 = (bf16[4,448,768]{2,1,0:T(8,128)(2,1)}, bf16[4,448,768]{2,1,0:T(8,128)(2,1)S(1)}, u32[]{:S(2)}) copy-start(bf16[4,448,768]{2,1,0:T(8,128)(2,1)S(1)} %get-tuple-element.41.hid) | copy-start | bytes 8257540
  60.0 1.4 copy-start.9
  61.4 1.3 copy-start.11
  62.7 1.0 copy-start.4
  62.7 1.1 copy-start.18
  69.2 1.8 %copy-start.8 = (bf16[4,448,768]{2,1,0:T(8,128)(2,1)S(1)}, bf16[4,448,768]{2,1,0:T(8,128)(2,1)}, u32[]{:S(2)}) copy-start(bf16[4,448,768]{2,1,0:T(8,128)(2,1)} %copy-done.7) | copy-start | bytes 8257540
  71.0 1.6 %copy-start.10 = (f32[16,64,448]{2,1,0:T(8,128)S(1)}, f32[16,64,448]{2,1,0:T(8,128)}, u32[]{:S(2)}) copy-start(f32[16,64,448]{2,1,0:T(8,128)} %copy-done.9) | copy-start | bytes 5505028
  72.6 1.5 %copy-start.12 = (bf16[4,448,512]{2,1,0:T(8,128)(2,1)S(1)}, bf16[4,448,512]{2,1,0:T(8,128)(2,1)}, u32[]{:S(2)}) copy-start(bf16[4,448,512]{2,1,0:T(8,128)(2,1)} %copy-done.11) | copy-start | bytes 5505028
  74.1 14.2 %copy-start.14 = (f32[256,1536]{1,0:T(8,128)S(1)}, f32[256,1536]{1,0:T(8,128)}, u32[]{:S(2)}) copy-start(f32[256,1536]{1,0:T(8,128)} %copy-done.13) | copy-start | bytes 4718596
  86.6 1.6 %copy-start.6 = (bf16[32,64,768]{2,1,0:T(8,128)(2,1)}, bf16[32,64,768]{2,1,0:T(8,128)(2,1)S(1)}, u32[]{:S(2)}) copy-start(bf16[32,64,768]{2,1,0:T(8,128)(2,1)S(1)} %get-tuple-element.44) | copy-start | bytes 9437188

commit v4 on v3

--- a/solution.py
+++ b/solution.py
@@ -632,7 +632,7 @@
 
     one_a.start()
     one_b.start()
-    lax.fori_loop(0, 4, launch, 0)
+    lax.fori_loop(0, 2, launch, 0)
 
     for load in loads:
         load.wait()
@@ -680,6 +680,7 @@
     two_b = remote(s1b.at[:, 1 - x], g2b, xs.at[3], xr.at[3], {"tok": xn})
     two_a.start()
     two_b.start()
+    lax.fori_loop(2, 4, launch, 0)
     pass_on(1)
     feed(1)
     pass_on(2)
@@ -688,7 +689,6 @@
         pmsg[b] = part[pl.ds(pl.multiple_of(b * per + other * half, half), half), :].astype(BF16)
     swap_part = remote(pmsg, pbox, xs.at[4], xr.at[4], {"mdl": other})
     swap_part.start()
-    pass_on(3)
     two_a.wait()
     two_b.wait()
     s2[:, :, 0:cut] = (s1a[:, y].astype(F32) + g2a[...].astype(F32)).astype(BF16)
@@ -701,6 +701,7 @@
         )
         copy.start()
         last.append(copy)
+    pass_on(3)
     swap_part.wait()
     for q in (1, 2, 3):
         plane_copy(q, 0).wait()
@@ -778,10 +779,12 @@
     def shape(dims, kind=BF16):
         return jax.ShapeDtypeStruct(dims, kind)
 
-    def talk(ident):
+    def talk(ident, room):
         return pltpu.CompilerParams(
-            vmem_limit_bytes=48 << 20, collective_id=ident, has_side_effects=True
+            vmem_limit_bytes=room << 20, collective_id=ident, has_side_effects=True
         )
+
+    small = pltpu.CompilerParams(vmem_limit_bytes=10 << 20)
 
     recv, hidden, packed, up_pre, part_ffn, table = pl.pallas_call(
         functools.partial(gather_kernel, devices),
@@ -808,7 +811,7 @@
             dma((devices - 1,)),
             dma((devices - 1,)),
         ],
-        compiler_params=talk(2),
+        compiler_params=talk(2, 48),
         name="gather",
     )(send, tokens, gain, row, w_qkv, w_up, w_down)
 
@@ -823,7 +826,7 @@
         in_specs=[SM] + [VM] * 7,
         out_specs=(VM,) * 4,
         scratch_shapes=[pltpu.VMEM((faces * per, width), BF16)],
-        compiler_params=PARAMS,
+        compiler_params=small,
         name="attend",
     )(arrival, hidden, packed, recv.reshape(total, per, width), gain, w_qkv, rel_bias, seen)
 
@@ -834,7 +837,7 @@
         in_specs=[VM] * 4,
         out_specs=(VM, VM),
         scratch_shapes=[pltpu.VMEM((rows, width), F32), dma, dma],
-        compiler_params=talk(0),
+        compiler_params=talk(0, 8),
         name="fold_swap",
     )(flat, part_out, cotangent.reshape(rows, width), w_disp)
     grad_mixed = jnp.dot(grad_out, w_out.T, preferred_element_type=F32).astype(BF16)
@@ -849,7 +852,7 @@
         in_specs=[SM] + [VM] * 6,
         out_specs=(VM,) * 3,
         scratch_shapes=[pltpu.VMEM((span, wide), BF16), pltpu.VMEM((width, wide), F32)],
-        compiler_params=PARAMS,
+        compiler_params=small,
         name="attend_back",
     )(arrival, packed, window, hid, probs, grad_mixed, w_qkv)
 
@@ -890,7 +893,7 @@
             dma((3,)),
             dma((3,)),
         ],
-        compiler_params=talk(1),
+        compiler_params=talk(1, 48),
         name="give_back",
     )(
         table[:, 0, : devices * slots].reshape(-1),

time: 145 us -> 145 us (level)
  no operation moved by 1% of the time
where the time goes in v4:
time: 145 us; the launch traced here: 143 us
  Pallas kernels  116 us (80%)
  local copies, waits for them, and re-layouts  25 us (17%)
    pallas_call x1, Pallas kernels, body(): pl.pallas_call(functools.partial(return_kernel, devices), out_shape=(shap...  54.7 us
    pallas_call x1, Pallas kernels, body(): pl.pallas_call(functools.partial(gather_kernel, devices), out_shape=(shap...  36.5 us
    unnamed x42, local copies, waits for them, and re-layouts  21.1 us
    pallas_call x1, Pallas kernels, body(): pl.pallas_call(functools.partial(attend_back_kernel, heads, dh, per, face...  12.5 us
    pallas_call x1, Pallas kernels, body(): pl.pallas_call(functools.partial(attend_kernel, heads, dh, per, faces), o...  9.19 us
    pallas_call x1, Pallas kernels, body(): pl.pallas_call(fold_swap_kernel, out_shape=(shape((1, rows), F32), shape(...  3.3 us

profile of v4, /device:TPU:0, one launch (start us, length us, event | category | flops | bytes accessed | tf_op | source)
XLA Modules:
  0.0 143.5 jit_solution(6890066204864173098)
XLA Ops:
  0.6 0.8 reshape.74
  1.6 0.8 concatenate.5
  2.4 0.7 reshape.72.gain
  3.1 0.8 copy.21
  4.2 1.1 copy.23.w_disp
  5.3 1.3 copy-done.1
  6.6 1.0 copy-done.3
  7.6 36.5 %gather.1 = (bf16[16,2,64,768]{3,2,1,0:T(8,128)(2,1)}, bf16[256,768]{1,0:T(8,128)(2,1)S(1)}, bf16[256,768]{1,0:T(8,128)(2,1)S(1)}, f32[256,1536]{1,0:T(8,128)S(1...) custom-call(s32[32]{0:T(128)S(1)} %reshape.71.send, bf16[4,64,768]{2,1,0:T(8,128)(2,1)S(1)} %copy-done.3, ...), custom_call_target="tpu_custom_call" | custom-call | tf_op jit(solution)/shard_map/gather/pallas_call | solution.py:789
  44.2 1.2 copy-done.13
  45.3 0.9 copy-done.15
  46.4 1.9 %copy-done.5 = bf16[16,2,64,768]{3,2,1,0:T(8,128)(2,1)S(1)} copy-done((bf16[16,2,64,768]{3,2,1,0:T(8,128)(2,1)S(1)}, bf16[16,2,64,768]{3,2,1,0:T(8,128)(2,1)}, u32[]{:S(2)}) %copy-start.5) | copy-done | bytes 3145752
  48.3 1.0 copy-done.17
  49.3 9.2 %attend.1 = (bf16[256,256]{1,0:T(8,128)(2,1)S(1)}, f32[16,64,448]{2,1,0:T(8,128)S(1)}, bf16[4,448,512]{2,1,0:T(8,128)(2,1)S(1)}, bf16[4,448,768]{2,1,0:T(8,128)(2,1)S(1)}) custom-call(s32[24]{0:T(128)S(1)} %multiply_add_fusion.arrival, bf16[256,768]{1,0:T(8,128)(2,1)S(1)} %get-tuple-element.33.hidden, bf16[256,768]{1,0:T(8,128)(2,1)S(1)} %get-tuple-element.34.packed, ...), custom_call_target="tpu_custom_call" | custom-call | tf_op jit(solution)/shard_map/attend/pallas_call | solution.py:818
  58.5 1.4 copy-done.9
  59.9 1.3 copy-done.11
  61.5 1.0 copy-done.4
  62.8 3.3 %fold_swap.1 = (f32[1,256]{1,0:T(1,128)S(1)}, bf16[256,768]{1,0:T(8,128)(2,1)S(1)}) custom-call(bf16[256,768]{1,0:T(8,128)(2,1)S(1)} %bitcast.9, f32[256,768]{1,0:T(8,128)S(1)} %convolution_add_fusion.part, bf16[256,768]{1,0:T(8,128)(2,1)S(1)} %bitcast.13, bf16[768,192]{1,0:T(8,128)(2,1)S(1)} %copy.23.w_disp), custom_call_target="tpu_custom_call" | custom-call | tf_op jit(solution)/shard_map/fold_swap/pallas_call | solution.py:834
  68.3 1.8 %copy-done.8 = bf16[4,448,768]{2,1,0:T(8,128)(2,1)S(1)} copy-done((bf16[4,448,768]{2,1,0:T(8,128)(2,1)S(1)}, bf16[4,448,768]{2,1,0:T(8,128)(2,1)}, u32[]{:S(2)}) %copy-start.8) | copy-done | bytes 2752536
  70.1 1.6 %copy-done.10 = f32[16,64,448]{2,1,0:T(8,128)S(1)} copy-done((f32[16,64,448]{2,1,0:T(8,128)S(1)}, f32[16,64,448]{2,1,0:T(8,128)}, u32[]{:S(2)}) %copy-start.10) | copy-done | bytes 1835032
  71.7 1.5 %copy-done.12 = bf16[4,448,512]{2,1,0:T(8,128)(2,1)S(1)} copy-done((bf16[4,448,512]{2,1,0:T(8,128)(2,1)S(1)}, bf16[4,448,512]{2,1,0:T(8,128)(2,1)}, u32[]{:S(2)}) %copy-start.12) | copy-done | bytes 1835032
  73.2 12.5 %attend_back.1 = (f32[256,768]{1,0:T(8,128)S(1)}, bf16[32,64,768]{2,1,0:T(8,128)(2,1)S(1)}, bf16[768,768]{1,0:T(8,128)(2,1)S(1)}) custom-call(s32[24]{0:T(128)S(1)} %multiply_add_fusion.arrival, bf16[256,768]{1,0:T(8,128)(2,1)S(1)} %get-tuple-element.34.packed, bf16[4,448,512]{2,1,0:T(8,128)(2,1)S(1)} %copy-done.12, bf16[4,448,768]{2,1,0:T(8,128)(2,1)S(1)} %copy-done.8, ...), custom_call_target="tpu_custom_call" | custom-call | tf_op jit(solution)/shard_map/attend_back/pallas_call | solution.py:845
  85.7 1.6 %copy-done.6 = bf16[32,64,768]{2,1,0:T(8,128)(2,1)} copy-done((bf16[32,64,768]{2,1,0:T(8,128)(2,1)}, bf16[32,64,768]{2,1,0:T(8,128)(2,1)S(1)}, u32[]{:S(2)}) %copy-start.6) | copy-done | bytes 3145752
  87.3 54.7 %give_back.1 = (bf16[4,64,768]{2,1,0:T(8,128)(2,1)S(1)}, f32[48,768]{1,0:T(8,128)S(1)}) custom-call(s32[512]{0:T(512)S(1)} %reshape_squeeze.3.send, bf16[4,64,768]{2,1,0:T(8,128)(2,1)S(1)} %copy-done.4, f32[1,768]{1,0:T(1,128)S(1)} %reshape.72.gain, bf16[256,768]{1,0:T(8,128)(2,1)S(1)} %get-tuple-element.39.gout, f32[256,768]{1,0:T(8,128)S(1)} %get-tuple-element.43.own, ...), custom_call_target="tpu_custom_call" | custom-call | tf_op jit(solution)/shard_map/give_back/pallas_call | solution.py:861
  142.1 0.7 copy.26
  (40 shorter events, 4.1 us)
Async XLA Ops:
  0.6 60.5 %copy-start = (bf16[256,768]{1,0:T(8,128)(2,1)S(1)}, bf16[256,768]{1,0:T(8,128)(2,1)}, u32[]{:S(2)}) copy-start(bf16[256,768]{1,0:T(8,128)(2,1)} %param.18) | copy-start | bytes 1179652
  5.3 1.3 copy-start.1
  6.6 1.0 copy-start.3
  7.6 38.8 %copy-start.2 = (bf16[768,768]{1,0:T(8,128)(2,1)S(1)}, bf16[768,768]{1,0:T(8,128)(2,1)}, u32[]{:S(2)}) copy-start(bf16[768,768]{1,0:T(8,128)(2,1)} %wq.3) | copy-start | bytes 3538948
  44.1 1.2 copy-start.13
  45.3 0.9 copy-start.15
  46.4 1.9 %copy-start.5 = (bf16[16,2,64,768]{3,2,1,0:T(8,128)(2,1)S(1)}, bf16[16,2,64,768]{3,2,1,0:T(8,128)(2,1)}, u32[]{:S(2)}) copy-start(bf16[16,2,64,768]{3,2,1,0:T(8,128)(2,1)} %get-tuple-element.35) | copy-start | bytes 9437188
  48.3 1.0 copy-start.17
  49.3 11.9 %copy-start.16 = (f32[256,768]{1,0:T(8,128)S(1)}, f32[256,768]{1,0:T(8,128)}, u32[]{:S(2)}) copy-start(f32[256,768]{1,0:T(8,128)} %copy-done.15) | copy-start | bytes 2359300
  58.5 1.4 copy-start.9
  59.9 1.3 copy-start.11
  61.2 5.0 %copy-start.7 = (bf16[4,448,768]{2,1,0:T(8,128)(2,1)}, bf16[4,448,768]{2,1,0:T(8,128)(2,1)S(1)}, u32[]{:S(2)}) copy-start(bf16[4,448,768]{2,1,0:T(8,128)(2,1)S(1)} %get-tuple-element.41.hid) | copy-start | bytes 8257540
  61.2 1.3 copy-start.4
  61.2 1.7 %copy-start.18 = (bf16[4,64,768]{2,1,0:T(8,128)(2,1)S(1)}, bf16[4,64,768]{2,1,0:T(8,128)(2,1)}, u32[]{:S(2)}) copy-start(bf16[4,64,768]{2,1,0:T(8,128)(2,1)} %param.15) | copy-start | bytes 1179652
  68.3 1.8 %copy-start.8 = (bf16[4,448,768]{2,1,0:T(8,128)(2,1)S(1)}, bf16[4,448,768]{2,1,0:T(8,128)(2,1)}, u32[]{:S(2)}) copy-start(bf16[4,448,768]{2,1,0:T(8,128)(2,1)} %copy-done.7) | copy-start | bytes 8257540
  70.1 1.6 %copy-start.10 = (f32[16,64,448]{2,1,0:T(8,128)S(1)}, f32[16,64,448]{2,1,0:T(8,128)}, u32[]{:S(2)}) copy-start(f32[16,64,448]{2,1,0:T(8,128)} %copy-done.9) | copy-start | bytes 5505028
  71.7 1.5 %copy-start.12 = (bf16[4,448,512]{2,1,0:T(8,128)(2,1)S(1)}, bf16[4,448,512]{2,1,0:T(8,128)(2,1)}, u32[]{:S(2)}) copy-start(bf16[4,448,512]{2,1,0:T(8,128)(2,1)} %copy-done.11) | copy-start | bytes 5505028
  73.2 14.2 %copy-start.14 = (f32[256,1536]{1,0:T(8,128)S(1)}, f32[256,1536]{1,0:T(8,128)}, u32[]{:S(2)}) copy-start(f32[256,1536]{1,0:T(8,128)} %copy-done.13) | copy-start | bytes 4718596
  85.7 1.6 %copy-start.6 = (bf16[32,64,768]{2,1,0:T(8,128)(2,1)}, bf16[32,64,768]{2,1,0:T(8,128)(2,1)S(1)}, u32[]{:S(2)}) copy-start(bf16[32,64,768]{2,1,0:T(8,128)(2,1)S(1)} %get-tuple-element.44) | copy-start | bytes 9437188
